TPU v7x, 32 devices: a whole 2x2x4 slice. The times are simulated.
32 devices in a mesh: row: 4 (over y, core), col: 8 (over z, x).
Axes of the slice: x: 2, y: 2, z: 4, core: 2. Of those that a mesh axis runs over, the one named last changes fastest.
Arguments:
- front: float32 [12288, 12288], P('row', 'col'), may hold values from -6 to 6
- delayed: float32 [64, 12288], P('col', 'row'), may hold values from -6 to 6
- dest: int32 [64], P('col'), may hold values from 0 to 1023, as said below
- pivots: int32 [1024], replicated, may hold values from 0 to 12287, as said below
- pair_flags: int32 [1024], replicated, may hold values from 0 to 1, as said below
- linv: float32 [4, 256, 256], replicated, as said below
- dinv_diag: float32 [1024], replicated, may hold values from -0.1 to 0.1
- dinv_off: float32 [1024], replicated, may hold values from -0.08 to 0.08
Outputs:
- trailing: float32 [12288, 12288], P('row', 'col')
- factor: float32 [12288, 1024], P('row')
Inputs may be any that keep to these rules, and one draw needn't show every extreme that they name: Distinct front columns; slots p * 256 to (p + 1) * 256 - 1 are panel p's pivots. Each block of 1536 columns held by one index of col contains exactly 128 of them. `pair_flags`: A 1 at slot s joins slots s and s + 1 into one 2x2 block; no two 1s are adjacent and the last slot of a panel holds 0. `dest`: several delayed columns may share a slot. Of the 8 delayed columns held by one index of col, at most 2 go to pivot columns held by the same index of col. `linv`: each panel's matrix is unit lower triangular: ones on the diagonal, zeros above it.
All inputs are finite; a program needn't handle non-finite values.
Results may differ from a plain program's by a relative error of at most 0.00015.
Values sent between devices are 32-bit elements; how exact they have to be, the bound alone decides.
A program may use at most 192 MiB of HBM per device.

v0:
```python
import functools

import jax
import jax.numpy as jnp
from jax import lax
from jax.experimental import pallas as pl
from jax.experimental.pallas import tpu as pltpu
from jax.sharding import PartitionSpec as P

MESH = pl.DeviceIdType.MESH
VMEM_LIMIT = 60 * 1024 * 1024


def dot(a, b, ca, cb):
    return lax.dot_general(a, b, (((ca,), (cb,)), ((), ())), precision=lax.Precision.HIGHEST)


def pick(ones, a, c1, ca):
    total = None
    for _ in range(3):
        part = lax.reduce_precision(a, 8, 7)
        a = a - part
        term = lax.dot_general(
            ones.astype(jnp.bfloat16), part.astype(jnp.bfloat16), (((c1,), (ca,)), ((), ())),
            preferred_element_type=jnp.float32,
        )
        total = term if total is None else total + term
    return total


def onehot(a, b):
    return (a[:, None] == b[None, :]).astype(jnp.float32)


def pair_scale(scaled, panel_width, pair_flags, diag_part, off_part):
    total = scaled.shape[1]
    slot = lax.broadcasted_iota(jnp.int32, (total,), 0) % panel_width
    coupled = pair_flags.astype(jnp.float32) * off_part
    up = jnp.where(slot == panel_width - 1, 0.0, coupled)
    down = jnp.where(slot == 0, 0.0, jnp.roll(coupled, 1))
    nxt = jnp.roll(scaled, -1, axis=1)
    prv = jnp.roll(scaled, 1, axis=1)
    return scaled * diag_part + nxt * up + prv * down


def gather_kernel(zs, xs, ys, halves, own_ref, all_ref, col_ref, copy_sem, root_sem, all_send, all_recv, col_send, col_recv):
    row, col = lax.axis_index("row"), lax.axis_index("col")
    y, k = row // 2, row % 2
    z, x = col // xs, col % xs
    root = col // halves
    half = col % halves
    root_y, root_k = root // 2, root % 2
    is_root = row == root
    at_root_core = k == root_k

    def at(y_, k_, z_, x_):
        return (y_ * 2 + k_, z_ * xs + x_)

    links = [
        (z + 1 < zs, at(y, k, z + 1, x)),
        (z >= 1, at(y, k, z - 1, x)),
        (x + 1 < xs, at(y, k, z, x + 1)),
        (x >= 1, at(y, k, z, x - 1)),
        (y + 1 < ys, at(y + 1, k, z, x)),
        (y >= 1, at(y - 1, k, z, x)),
        (True, at(y, 1 - k, z, x)),
    ]

    def when(cond, fn):
        if cond is True:
            fn()
        else:
            pl.when(cond)(fn)

    barrier = pltpu.get_barrier_semaphore()
    for cond, dev in links:
        when(cond, lambda dev=dev: pl.semaphore_signal(barrier, inc=1, device_id=dev, device_id_type=MESH))
    peers = 1
    for cond, _ in links[:6]:
        peers = peers + jnp.where(cond, 1, 0)
    pl.semaphore_wait(barrier, peers)

    def block(b, c):
        return all_ref.at[b, c]

    def send_all(way, b, c, src, act):
        act(pltpu.make_async_remote_copy(
            src_ref=src, dst_ref=block(b, c), send_sem=all_send.at[way, b, c], recv_sem=all_recv.at[b, c],
            device_id=links[way][1], device_id_type=MESH))

    def send_col(way, c, src, act):
        act(pltpu.make_async_remote_copy(
            src_ref=src, dst_ref=col_ref.at[c], send_sem=col_send.at[way, c], recv_sem=col_recv.at[c],
            device_id=links[4 + way][1], device_id_type=MESH))

    def arrived(b, c):
        pltpu.make_async_copy(block(b, c), block(b, c), all_recv.at[b, c]).wait()

    def spread_col(c, src, up, down, act):
        when((y + 1 < ys) & up, lambda: send_col(0, c, src, act))
        when((y >= 1) & down, lambda: send_col(1, c, src, act))
        send_col(2, c, src, act)

    def on_block(c, mine, act, draining):
        def go():
            src = own_ref.at[half] if mine else block(half, c)
            spread_col(c, src, True, True, act)
            local = pltpu.make_async_copy(src, col_ref.at[c], root_sem.at[c])
            if draining:
                local.wait()
            else:
                local.start()
        when(is_root, go)

    def on_col(c, act, draining):
        def go():
            if not draining:
                pltpu.make_async_copy(col_ref.at[c], col_ref.at[c], col_recv.at[c]).wait()
            spread_col(c, col_ref.at[c], y > root_y, y < root_y, act)
        when(at_root_core & (y != root_y), go)

    def steps(act, draining):
        pending = []

        def later(cond, c):
            pending.append((cond, c))
            if len(pending) > 3:
                flush()

        def flush():
            cond, c = pending.pop(0)
            when(cond, lambda: on_col(c, act, draining))

        for t in range(zs + xs - 1):
            if t < zs:
                for sign in ((0,) if t == 0 else (-1, 1)):
                    zc = z + sign * t
                    here = True if t == 0 else (zc >= 0) & (zc < zs)
                    c = zc * xs + x

                    def go(c=c, sign=sign, t=t):
                        for b in range(halves):
                            if t and not draining:
                                arrived(b, c)
                            src = own_ref.at[b] if t == 0 else block(b, c)
                            when(x + 1 < xs, lambda: send_all(2, b, c, src, act))
                            when(x >= 1, lambda: send_all(3, b, c, src, act))
                            if sign <= 0:
                                when(z + 1 < zs, lambda: send_all(0, b, c, src, act))
                            if sign >= 0:
                                when(z >= 1, lambda: send_all(1, b, c, src, act))
                        on_block(c, t == 0, act, draining)
                    when(here, go)
                    later(here, c)
            for d in range(1, xs):
                tz = t - d
                if tz < 0 or tz >= zs:
                    continue
                for sign in ((0,) if tz == 0 else (-1, 1)):
                    for side in (-1, 1):
                        zc, xc = z + sign * tz, x + side * d
                        here = (zc >= 0) & (zc < zs) & (xc >= 0) & (xc < xs)
                        c = zc * xs + xc

                        def go(c=c, side=side):
                            for b in range(halves):
                                if not draining:
                                    arrived(b, c)
                                if side < 0:
                                    when(x + 1 < xs, lambda: send_all(2, b, c, block(b, c), act))
                                else:
                                    when(x >= 1, lambda: send_all(3, b, c, block(b, c), act))
                            on_block(c, False, act, draining)
                        when(here, go)
                        later(here, c)
        while pending:
            flush()

    keep = [pltpu.make_async_copy(own_ref.at[b], block(b, col), copy_sem.at[b]) for b in range(halves)]
    for copy in keep:
        copy.start()
    steps(lambda copy: copy.start(), False)
    for copy in keep:
        copy.wait()
    steps(lambda copy: copy.wait_send(), True)

    def last():
        for c in range(zs * xs):
            pltpu.make_async_copy(col_ref.at[c], col_ref.at[c], col_recv.at[c]).wait()
    when(k != root_k, last)


def exchange(own, halves, height):
    n_col = lax.axis_size("col")
    n_row = lax.axis_size("row")
    slots = own.shape[1]
    ys = n_row // 2
    xs = ys if n_col % ys == 0 else 1
    zs = n_col // xs
    vmem = pl.BlockSpec(memory_space=pltpu.VMEM)
    every, cols = pl.pallas_call(
        functools.partial(gather_kernel, zs, xs, ys, halves),
        out_shape=(
            jax.ShapeDtypeStruct((halves, n_col, height, slots), jnp.float32),
            jax.ShapeDtypeStruct((n_col, height, slots), jnp.float32),
        ),
        in_specs=[vmem],
        out_specs=(vmem, vmem),
        scratch_shapes=[
            pltpu.SemaphoreType.DMA((halves,)),
            pltpu.SemaphoreType.DMA((n_col,)),
            pltpu.SemaphoreType.DMA((4, halves, n_col)),
            pltpu.SemaphoreType.DMA((halves, n_col)),
            pltpu.SemaphoreType.DMA((3, n_col)),
            pltpu.SemaphoreType.DMA((n_col,)),
        ],
        compiler_params=pltpu.CompilerParams(
            collective_id=0, has_side_effects=True, vmem_limit_bytes=VMEM_LIMIT
        ),
    )(own.reshape(halves, height, slots))
    return every.reshape(halves * n_col * height, slots), cols.reshape(n_col * height, slots)


def trailing_kernel(tile, s_ref, c_ref, front_ref, rkeep_ref, ckeep_ref, coef_ref, out_ref, factor_ref, chi, clo):
    slots = s_ref.shape[1]
    cols = c_ref.shape[0]

    @pl.when(pl.program_id(0) == 0)
    def _():
        @pl.loop(0, cols // tile)
        def _(i):
            part = pl.ds(pl.multiple_of(i * tile, tile), tile)
            block = c_ref[part, :].T
            hi = block.astype(jnp.bfloat16)
            chi[:, part] = hi
            clo[:, part] = (block - hi.astype(jnp.float32)).astype(jnp.bfloat16)

    s = s_ref[...]
    columns = (
        s * coef_ref[0:1, :]
        + pltpu.roll(s, slots - 1, 1) * coef_ref[1:2, :]
        + pltpu.roll(s, 1, 1) * coef_ref[2:3, :]
    )
    factor_ref[...] = columns
    hi = columns.astype(jnp.bfloat16)
    lo = (columns - hi.astype(jnp.float32)).astype(jnp.bfloat16)
    rkeep = rkeep_ref[...] > 0.0

    @pl.loop(0, cols // tile)
    def _(i):
        part = pl.ds(pl.multiple_of(i * tile, tile), tile)
        bh, bl = chi[:, part], clo[:, part]
        acc = jnp.dot(hi, bh, preferred_element_type=jnp.float32)
        acc += jnp.dot(hi, bl, preferred_element_type=jnp.float32)
        acc += jnp.dot(lo, bh, preferred_element_type=jnp.float32)
        out_ref[:, part] = jnp.where(rkeep & (ckeep_ref[:, part] > 0.0), front_ref[:, part] - acc, 0.0)


def update(every, col_scaled, front, row_keep, col_keep, coef):
    rows, cols = front.shape
    slots = every.shape[1]
    tile = 256
    return pl.pallas_call(
        functools.partial(trailing_kernel, tile),
        grid=(rows // tile,),
        in_specs=[
            pl.BlockSpec((tile, slots), lambda i: (i, 0)),
            pl.BlockSpec((cols, slots), lambda i: (0, 0)),
            pl.BlockSpec((tile, cols), lambda i: (i, 0)),
            pl.BlockSpec((tile, 1), lambda i: (i, 0)),
            pl.BlockSpec((1, cols), lambda i: (0, 0)),
            pl.BlockSpec((8, slots), lambda i: (0, 0)),
        ],
        out_specs=(
            pl.BlockSpec((tile, cols), lambda i: (i, 0)),
            pl.BlockSpec((tile, slots), lambda i: (i, 0)),
        ),
        out_shape=(
            jax.ShapeDtypeStruct((rows, cols), jnp.float32),
            jax.ShapeDtypeStruct((rows, slots), jnp.float32),
        ),
        scratch_shapes=[pltpu.VMEM((slots, cols), jnp.bfloat16), pltpu.VMEM((slots, cols), jnp.bfloat16)],
        compiler_params=pltpu.CompilerParams(
            dimension_semantics=("arbitrary",), vmem_limit_bytes=VMEM_LIMIT
        ),
    )(every, col_scaled, front, row_keep, col_keep, coef)


def body(front, delayed, dest, pivots, pair_flags, linv, dinv_diag, dinv_off):
    n_col = lax.axis_size("col")
    n_row = lax.axis_size("row")
    rows_blk, cols_blk = front.shape
    row_id = lax.axis_index("row")
    col_id = lax.axis_index("col")
    row_start = row_id * rows_blk
    col_start = col_id * cols_blk
    panels, width, _ = linv.shape
    slots = pivots.shape[0]
    per_col = slots // n_col
    per_row = slots // n_row
    ndel = delayed.shape[0]
    halves = rows_blk // cols_blk
    height = cols_blk // n_col
    slot_ids = jnp.arange(slots, dtype=jnp.int32)

    col_owner = pivots // cols_blk
    row_owner = pivots // rows_blk
    before = slot_ids[None, :] < slot_ids[:, None]
    col_rank = jnp.sum((before & (col_owner[:, None] == col_owner[None, :])).astype(jnp.int32), axis=1)
    row_rank = jnp.sum((before & (row_owner[:, None] == row_owner[None, :])).astype(jnp.int32), axis=1)
    col_rel = jnp.where(col_owner == col_id, pivots - col_start, -1)
    row_rel = jnp.where(row_owner == row_id, pivots - row_start, -1)
    col_want = jnp.sum(
        jnp.where((col_owner == col_id)[None, :] & (col_rank[None, :] == jnp.arange(per_col)[:, None]), col_rel[None, :], 0),
        axis=1,
    )
    row_want = jnp.sum(
        jnp.where((row_owner == row_id)[None, :] & (row_rank[None, :] == jnp.arange(per_row)[:, None]), row_rel[None, :], 0),
        axis=1,
    )

    picked = pick(onehot(col_want, jnp.arange(cols_blk)), front, 1, 1)
    mine = jnp.concatenate([picked, delayed], axis=0)
    wide = per_col + ndel

    piv_part = pick(onehot(row_want, jnp.arange(rows_blk)), mine, 1, 1).T
    slot_row = jnp.pad(dest.astype(jnp.float32)[None, :], ((0, 7), (0, per_row - ndel)))
    piv_all = lax.all_gather(jnp.concatenate([piv_part, slot_row], axis=0), ("row", "col"), axis=0, tiled=False)
    piv_all = piv_all.reshape(n_row, n_col, wide + 8, per_row)
    dest_all = piv_all[0, :, wide, :ndel].astype(jnp.int32)
    piv_all = piv_all[:, :, :wide].reshape(n_row, n_col * wide, per_row)
    share = mine.reshape(wide, halves, n_col, height).transpose(2, 0, 1, 3)
    share = share.reshape(n_col, wide, halves * height)
    share = lax.all_to_all(share, "col", split_axis=0, concat_axis=0, tiled=True)
    share = share.reshape(n_col * wide, halves * height)

    home = jnp.where(
        jnp.arange(wide)[None, :] < per_col,
        jnp.arange(n_col)[:, None] * per_col + jnp.arange(wide)[None, :],
        -1,
    )
    is_col = home.reshape(-1)[:, None] == (col_owner * per_col + col_rank)[None, :]
    dest_wide = jnp.concatenate([jnp.full((n_col, per_col), -1, jnp.int32), dest_all], axis=1)
    is_del = dest_wide.reshape(-1)[:, None] == slot_ids[None, :]
    take = (is_col | is_del).astype(jnp.float32)
    stacked = jnp.concatenate([piv_all[r] for r in range(n_row)] + [share], axis=1)
    current = dot(stacked, take, 0, 0)
    to_slot = onehot(row_owner * per_row + row_rank, slot_ids)

    done = []
    parts = []
    for p in range(panels):
        lo, hi = p * width, (p + 1) * width
        cols = current[:, lo:hi]
        for earlier_cols, earlier_rows, start in done:
            cols = cols - dot(earlier_cols, earlier_rows[lo - start : hi - start], 1, 1)
        scaled = dot(cols, linv[p], 1, 1)
        parts.append(scaled[slots:])
        if p + 1 < panels:
            columns = pair_scale(scaled, width, pair_flags[lo:hi], dinv_diag[lo:hi], dinv_off[lo:hi])
            rows = pick(to_slot[hi:], scaled[:slots], 1, 0)
            done.append((columns, rows, hi))
    own = jnp.concatenate(parts, axis=1)

    every, col_scaled = exchange(own, halves, height)
    in_panel = slot_ids % width
    coupled = pair_flags.astype(jnp.float32) * dinv_off
    zero = jnp.zeros_like(dinv_diag)
    coef = jnp.stack(
        [dinv_diag, jnp.where(in_panel == width - 1, 0.0, coupled), jnp.where(in_panel == 0, 0.0, jnp.roll(coupled, 1))]
        + [zero] * 5
    )
    row_in = jnp.any((row_start + jnp.arange(rows_blk))[:, None] == pivots[None, :], axis=1)
    col_in = jnp.any((col_start + jnp.arange(cols_blk))[:, None] == pivots[None, :], axis=1)
    row_keep = jnp.where(row_in, 0.0, 1.0)[:, None]
    col_keep = jnp.where(col_in, 0.0, 1.0)[None, :]
    trailing, factor = update(every, col_scaled, front, row_keep, col_keep, coef)
    return (trailing, factor)


def solution(mesh):
    return jax.shard_map(
        body,
        mesh=mesh,
        in_specs=(P("row", "col"), P("col", "row"), P("col"), P(), P(), P(), P(), P()),
        out_specs=(P("row", "col"), P("row", None)),
        check_vma=False,
    )
```

profile of v0, /device:TPU:5, one launch (start us, length us, event | category | flops | bytes accessed | tf_op | source)
XLA Modules:
  0.0 414.5 jit_solution(4496381067001617687)
XLA Ops:
  7.2 0.7 subtract_select_fusion.1
  7.9 2.3 convert_reduce_fusion
  10.5 9.6 %fusion.2 = f32[128,3072]{1,0:T(8,128)S(1)} fusion(f32[3072,1536]{1,0:T(8,128)} %front_ref.1, s32[128]{0:T(128)S(1)} %select_reduce_fusion.1), kind=kOutput, calls=%fused_computation.7 | convolution fusion | flops 1217986560 | bytes 20447744 | tf_op jit(solution)/shard_map/dot_general | solution.py:23
  20.1 8.1 %fusion.15 = f32[128,3072]{1,0:T(8,128)S(1)} fusion(f32[128,3072]{1,0:T(8,128)S(1)} %fusion.2, f32[3072,1536]{1,0:T(8,128)} %front_ref.1, s32[128]{0:T(128)S(1)} %select_reduce_fusion.1), kind=kOutput, calls=%fused_computation.23 | convolution fusion | flops 1227816960 | bytes 22020608 | tf_op jit(solution)/shard_map/dot_general | solution.py:23
  28.2 8.4 %fusion.12 = f32[128,3072]{1,0:T(8,128)S(1)} fusion(f32[128,3072]{1,0:T(8,128)S(1)} %fusion.15, f32[3072,1536]{1,0:T(8,128)} %front_ref.1, s32[128]{0:T(128)S(1)} %select_reduce_fusion.1), kind=kOutput, calls=%fused_computation.22 | convolution fusion | flops 1237254144 | bytes 22020608 | tf_op jit(solution)/shard_map/dot_general | solution.py:23
  36.6 0.3 select_reduce_fusion
  36.9 0.7 fusion.17
  37.7 0.8 fusion.16
  38.5 0.7 fusion.47
  39.2 0.7 select_maximum_fusion
  39.9 1.3 pad_maximum_fusion
  41.2 2.2 reshape.232
  43.5 2.5 copy.22
  46.0 4.1 reshape.233
  50.1 5.7 %all-to-all-start = ((f32[8,136,384]{2,1,0:T(8,128)}), f32[8,136,384]{2,1,0:T(8,128)S(1)}, u32[]{:S(2)}, u32[]{:S(2)}) async-start(f32[8,136,384]{2,1,0:T(8,128)} %reshape.233), calls=%async_computation | async-start | bytes 3342336 | tf_op jit(solution)/shard_map/all_to_all | solution.py:334
  55.9 1.0 compare_reduce_fusion.1
  56.9 2.0 compare_reduce_fusion
  59.1 0.6 select_n.171.ckeep_ref
  59.7 0.6 slice.246
  60.3 0.6 slice.207
  60.9 0.6 slice.223
  61.5 0.6 slice.240
  62.1 1.7 copy.19.rkeep_ref
  63.7 0.7 compare_select_fusion
  64.4 0.6 stack.16.coef_ref
  65.1 0.7 maximum_select_fusion
  65.8 0.7 maximum_select_fusion.1
  66.5 0.7 maximum_select_fusion.2
  67.2 1.7 convert_convert_fusion
  68.9 53.4 %all-gather.3.cloned.1.call-done = f32[4608,256]{1,0:T(8,128)} async-done(((f32[144,256]{1,0:T(8,128)}), f32[4608,256]{1,0:T(8,128)}) %all-gather.3.cloned.1.call-update) | async-done | bytes 4718608 | tf_op jit(solution)/shard_map/all_gather | solution.py:328
  122.3 0.8 slice.253
  123.2 2.7 fusion.101
  125.9 1.1 constant_dynamic-update-slice_fusion.4
  127.0 1.1 constant_dynamic-update-slice_fusion.3
  128.0 1.1 constant_dynamic-update-slice_fusion.2
  129.1 1.1 constant_dynamic-update-slice_fusion.1
  130.2 1.3 constant_dynamic-update-slice_fusion
  131.4 24.1 %fusion.7 = f32[1408,1024]{1,0:T(8,128)S(1)} fusion(f32[1088,1408]{1,0:T(8,128)} %constant_dynamic-update-slice_fusion, s32[1088]{0:T(1024)S(1)} %eq.233, s32[1024]{0:T(1024)S(1)} %multiply_add_fusion.1, s32[1088]{0:T(1024)S(1)} %select_n.160), kind=kOutput, calls=%fused_computation.13 | convolution fusion | flops 18827378688 | bytes 11907584 | tf_op jit(solution)/shard_map/dot_general | solution.py:15
  155.6 1.5 fusion.27
  157.3 2.2 copy-done.3
  159.6 0.6 fusion.44
  160.2 0.6 convolution_add_fusion.1
  160.8 0.6 convolution_add_fusion
  161.5 0.4 fusion.30
  161.9 2.5 fusion.78
  164.5 2.5 convolution_subtract_fusion.1
  167.0 2.8 convolution_subtract_fusion.2
  169.8 1.5 fusion.86
  171.3 0.5 fusion.58
  172.0 0.5 convolution_add_fusion.3
  172.5 0.5 convolution_add_fusion.2
  173.0 0.4 fusion.32
  173.4 2.5 fusion.76
  175.9 2.5 convolution_subtract_fusion
  178.5 1.5 fusion.84
  180.0 0.3 fusion.66
  180.6 0.3 convolution_add_fusion.5
  180.9 0.4 convolution_add_fusion.4
  181.3 3.0 fusion.35
  184.4 0.7 fusion.71
  185.0 0.3 slice-done
  185.7 1.6 copy.18
  187.3 160.1 %shard_map.95 = (f32[2,8,192,1024]{3,2,1,0:T(8,128)}, f32[8,192,1024]{2,1,0:T(8,128)}) custom-call(f32[2,192,1024]{2,1,0:T(8,128)} %bitcast.51), custom_call_target="tpu_custom_call" | custom-call | tf_op jit(solution)/shard_map/pallas_call | solution.py:201
  347.4 59.8 %shard_map.96 = (f32[3072,1536]{1,0:T(8,128)}, f32[3072,1024]{1,0:T(8,128)}) custom-call(f32[3072,1024]{1,0:T(8,128)} %bitcast.47, f32[1536,1024]{1,0:T(8,128)} %bitcast.50, f32[3072,1536]{1,0:T(8,128)} %front_ref.1, f32[3072,1]{1,0:T(8,128)} %copy.19.rkeep_ref, f32[1,1536]{1,0:T(1,128)} %select_n.171.ckeep_ref, f32[8,1024]{1,0:T(8,128)} %stack.16.coef_ref), custom_call_target="tpu_custom_call" | custom-call | tf_op jit(solution)/shard_map/pallas_call | solution.py:263
  (59 shorter events, 1.6 us)
Async XLA Ops:
  7.2 115.2 %all-gather.3.cloned.1.call-start = ((), (), s32[]{:S(2)}) async-start(), calls=%async_computation.1 | async-start | bytes 4866048 | tf_op jit(solution)/shard_map/all_gather | solution.py:328
  28.2 8.7 %copy-start.6 = (f32[8,3072]{1,0:T(8,128)S(1)}, f32[8,3072]{1,0:T(8,128)}, u32[]{:S(2)}) copy-start(f32[8,3072]{1,0:T(8,128)} %param.9) | copy-start | bytes 294916
  37.7 0.8 copy-start.11
  50.1 5.7 %copy-start.7 = (s32[1024]{0:T(1024)S(1)}, s32[1024]{0:T(1024)}, u32[]{:S(2)}) copy-start(s32[1024]{0:T(1024)} %param.11) | copy-start | bytes 12292
  50.1 8.7 %copy-start.9 = (f32[1024]{0:T(1024)S(1)}, f32[1024]{0:T(1024)}, u32[]{:S(2)}) copy-start(f32[1024]{0:T(1024)} %param.15) | copy-start | bytes 12292
  50.1 8.8 %copy-start.10 = (s32[1024]{0:T(1024)S(1)}, s32[1024]{0:T(1024)}, u32[]{:S(2)}) copy-start(s32[1024]{0:T(1024)} %param.12) | copy-start | bytes 12292
  50.1 8.8 %copy-start.8 = (f32[1024]{0:T(1024)S(1)}, f32[1024]{0:T(1024)}, u32[]{:S(2)}) copy-start(f32[1024]{0:T(1024)} %param.14) | copy-start | bytes 12292
  50.1 80.0 %all-to-all-start = ((f32[8,136,384]{2,1,0:T(8,128)}), f32[8,136,384]{2,1,0:T(8,128)S(1)}, u32[]{:S(2)}, u32[]{:S(2)}) async-start(f32[8,136,384]{2,1,0:T(8,128)} %reshape.233), calls=%async_computation | async-start | bytes 3342336 | tf_op jit(solution)/shard_map/all_to_all | solution.py:334
  131.4 24.1 %copy-start.5 = (f32[4,256,256]{2,1,0:T(8,128)S(1)}, f32[4,256,256]{2,1,0:T(8,128)}, u32[]{:S(2)}) copy-start(f32[4,256,256]{2,1,0:T(8,128)} %param.13) | copy-start | bytes 3145732
  155.5 11.4 %copy-start.4 = (f32[1408,1024]{1,0:T(8,128)}, f32[1408,1024]{1,0:T(8,128)S(1)}, u32[]{:S(2)}) copy-start(f32[1408,1024]{1,0:T(8,128)S(1)} %fusion.7) | copy-start | bytes 17301508
  157.1 4.4 %copy-start.2 = (f32[1408,256]{0,1:T(8,128)}, f32[1408,256]{0,1:T(8,128)S(1)}, u32[]{:S(2)}) copy-start(f32[1408,256]{0,1:T(8,128)S(1)} %fusion.27) | copy-start | bytes 4325380
  157.1 2.5 copy-start.3
  171.3 1.7 copy-start.1
  180.0 1.3 copy-start
  181.3 3.0 slice-start.3
  184.3 1.0 slice-start
  184.4 1.1 slice-start.1
  184.4 1.2 slice-start.2
Sparse Core Ops, SparseCore 0:
  40.1 82.2 all-gather.2
where the time goes:
time: 423 us; the launch traced here: 415 us
  Pallas kernels  220 us (52%)
  matrix products  77.9 us (18%)
  waiting for transfers between devices  53.4 us (13%)
  local copies, waits for them, and re-layouts  28.5 us (7%)
  between operations  15 us (4%)
  other arithmetic  14.1 us (3%)
  starting transfers between devices  5.71 us (1%)
    pallas_call x1, Pallas kernels, exchange(): pl.pallas_call(functools.partial(gather_kernel, zs, xs, ys, halves), out_...  160 us
    pallas_call x1, Pallas kernels, update(): pl.pallas_call(functools.partial(trailing_kernel, tile), grid=(rows // ti...  59.8 us
    all_gather x1, waiting for transfers between devices, body(): lax.all_gather(jnp.concatenate([piv_part, slot_row], axis=0), ('row', 'co...  53.4 us
    dot_general x11, matrix products, dot(): lax.dot_general(a, b, (((ca,), (cb,)), ((), ())), precision=lax.Precision...  45.1 us
    dot_general x15, matrix products, pick(): lax.dot_general(ones.astype(jnp.bfloat16), part.astype(jnp.bfloat16), (((...  32.8 us
  transfers between devices with their start and end apart: 2, of which 1 were waited for; matrix products, arithmetic and copies ran while one was open for 7% of the time, Pallas kernels for 0%

commit v1 on v0

v1 whole, which is shorter than its diff:
```python
import functools

import jax
import jax.numpy as jnp
from jax import lax
from jax.experimental import pallas as pl
from jax.experimental.pallas import tpu as pltpu
from jax.sharding import PartitionSpec as P

MESH = pl.DeviceIdType.MESH
VMEM_LIMIT = 62 * 1024 * 1024
F32 = jnp.float32
BF16 = jnp.bfloat16
CHUNK = 256
LANES = 128


def split(a):
    hi = a.astype(BF16)
    return hi, (a - hi.astype(F32)).astype(BF16)


def mm(a, b):
    return lax.dot_general(a, b, (((1,), (0,)), ((), ())), preferred_element_type=F32)


def mm_t(a, b):
    return lax.dot_general(a, b, (((1,), (1,)), ((), ())), preferred_element_type=F32)


def iota(shape, dim):
    return lax.broadcasted_iota(jnp.int32, shape, dim)


def one_hot(mask):
    return jnp.where(mask, 1.0, 0.0).astype(BF16)


def pick_kernel(front_ref, delayed_ref, dest_ref, irow_ref, icol_ref, raw_ref, piv_ref, g_ref, rowsel_ref, acc_ref, dacc_ref):
    i = pl.program_id(0)
    slots = irow_ref.shape[1]
    cols, wide = g_ref.shape
    per_row = rowsel_ref.shape[0]
    nd = delayed_ref.shape[0]
    ch = front_ref.shape[0]

    @pl.when(i == 0)
    def _():
        y = one_hot(icol_ref[:, 1:2] == iota((slots, wide), 1))

        @pl.loop(0, cols // CHUNK)
        def _(t):
            part = pl.ds(pl.multiple_of(t * CHUNK, CHUNK), CHUNK)
            x = one_hot(irow_ref[0:1, :] == iota((CHUNK, slots), 0) + t * CHUNK)
            g_ref[part, :] = mm(x, y).astype(BF16)

        rowsel_ref[...] = one_hot(irow_ref[1:2, :] == iota((per_row, slots), 0))
        acc_ref[...] = jnp.zeros_like(acc_ref)
        dacc_ref[...] = jnp.zeros_like(dacc_ref)

    hi, lo = split(front_ref[...])
    g = g_ref[...]
    raw = mm(hi, g) + mm(lo, g)
    raw_ref[0, :ch, :] = raw
    for b in range(ch // LANES):
        raw_ref[0, ch + b * nd : ch + (b + 1) * nd, :] = delayed_ref[:, b * LANES : (b + 1) * LANES]

    here = one_hot(icol_ref[:, 0:1] == iota((slots, ch), 1) + i * ch)
    sel = mm(rowsel_ref[...], here).astype(BF16)
    rh, rl = split(raw)
    acc_ref[...] += mm(sel, rh) + mm(sel, rl)
    dh, dl = split(delayed_ref[...])
    dacc_ref[...] += mm_t(dh, sel) + mm_t(dl, sel)

    @pl.when(i == pl.num_programs(0) - 1)
    def _():
        piv_ref[:per_row, :] = acc_ref[...]
        for b in range(per_row // LANES):
            piv_ref[per_row + b * nd : per_row + (b + 1) * nd, :] = dacc_ref[:, b * LANES : (b + 1) * LANES]
        piv_ref[per_row + per_row // LANES * nd :, :] = dest_ref[...]


def pick_columns(front, delayed, dest, irow, icol, wide, per_row):
    rows, cols = front.shape
    nd = delayed.shape[0]
    slots = irow.shape[1]
    n = rows // CHUNK
    high = CHUNK + nd * (CHUNK // LANES)
    piv_high = per_row + nd * (per_row // LANES) + nd
    return pl.pallas_call(
        pick_kernel,
        grid=(n,),
        in_specs=[
            pl.BlockSpec((CHUNK, cols), lambda i: (i, 0)),
            pl.BlockSpec((nd, CHUNK), lambda i: (0, i)),
            pl.BlockSpec((nd, wide), lambda i: (0, 0)),
            pl.BlockSpec((8, slots), lambda i: (0, 0)),
            pl.BlockSpec((slots, 8), lambda i: (0, 0)),
        ],
        out_specs=(
            pl.BlockSpec((1, high, wide), lambda i: (i, 0, 0)),
            pl.BlockSpec((piv_high, wide), lambda i: (0, 0)),
        ),
        out_shape=(
            jax.ShapeDtypeStruct((n, high, wide), F32),
            jax.ShapeDtypeStruct((piv_high, wide), F32),
        ),
        scratch_shapes=[
            pltpu.VMEM((cols, wide), BF16),
            pltpu.VMEM((per_row, slots), BF16),
            pltpu.VMEM((per_row, wide), F32),
            pltpu.VMEM((nd, per_row), F32),
        ],
        compiler_params=pltpu.CompilerParams(dimension_semantics=("arbitrary",), vmem_limit_bytes=VMEM_LIMIT),
    )(front, delayed, dest, irow, icol)


def gather_kernel(
    dims, raw_own, piv_own, linv_ref, coef_ref, irow_ref, icol_ref,
    cols_out, hi_out, lo_out,
    raw_all, col_raw, piv_all, rowperm, t1h, t1l, qh, ql, nh, nl, rd, mh, ml, stage, stage_h, stage_l,
    keep_sem, root_sem, raw_recv, raw_send, col_recv, col_send, piv_recv, piv_send, out_sem, hi_sem, lo_sem,
):
    zs, xs, ys, halves, per_row, nd, x_first = dims
    nc, n_row = zs * xs, ys * 2
    nch = raw_own.shape[0]
    high = raw_own.shape[1]
    hch = nch // halves
    panels, width, _ = linv_ref.shape
    slots = panels * width
    wide = raw_own.shape[2]
    ch = CHUNK
    kraw = nc * wide
    kall = mh.shape[0]
    row, col = lax.axis_index("row"), lax.axis_index("col")
    y, k = row // 2, row % 2
    z, x = col // xs, col % xs
    root = col // halves
    half = col % halves
    root_y, root_k = root // 2, root % 2
    is_root = row == root
    at_root_core = k == root_k
    reach = zs + xs - 2
    span = reach + ys - 1

    def at(y_, k_, z_, x_):
        return (y_ * 2 + k_, z_ * xs + x_)

    links = [
        (z + 1 < zs, at(y, k, z + 1, x)),
        (z >= 1, at(y, k, z - 1, x)),
        (x + 1 < xs, at(y, k, z, x + 1)),
        (x >= 1, at(y, k, z, x - 1)),
        (y + 1 < ys, at(y + 1, k, z, x)),
        (y >= 1, at(y - 1, k, z, x)),
        (None, at(y, 1 - k, z, x)),
    ]

    barrier = pltpu.get_barrier_semaphore()
    peers = 1
    for cond, dev in links:
        if cond is None:
            pl.semaphore_signal(barrier, inc=1, device_id=dev, device_id_type=MESH)
        else:
            peers = peers + jnp.where(cond, 1, 0)

            @pl.when(cond)
            def _(dev=dev):
                pl.semaphore_signal(barrier, inc=1, device_id=dev, device_id_type=MESH)
    pl.semaphore_wait(barrier, peers)

    def remote(way, src, dst, send, recv):
        return pltpu.make_async_remote_copy(
            src_ref=src, dst_ref=dst, send_sem=send, recv_sem=recv, device_id=links[way][1], device_id_type=MESH)

    def piv_ways(sy, c):
        zc, xc = c // xs, c % xs
        same_y = sy == y
        same_x = xc == x
        return [
            (0, (z + 1 < zs) & (zc <= z) & same_x & same_y),
            (1, (z >= 1) & (zc >= z) & same_x & same_y),
            (2, (x + 1 < xs) & (xc <= x) & same_y),
            (3, (x >= 1) & (xc >= x) & same_y),
            (4, (y + 1 < ys) & (sy <= y)),
            (5, (y >= 1) & (sy >= y)),
        ]

    def piv_copy(way, sy, c, src):
        s = sy * 2 + k
        return remote(way, src, piv_all.at[s, c], piv_send.at[way, sy * nc + c], piv_recv.at[s, c])

    def piv_arrived(s, c):
        pltpu.make_async_copy(piv_all.at[s, c], piv_all.at[s, c], piv_recv.at[s, c]).wait()

    def piv_step(sy, c, src):
        for way, cond in piv_ways(sy, c):
            @pl.when(cond)
            def _(way=way):
                piv_copy(way, sy, c, src).start()
        piv_copy(6, sy, c, src).start()

    def raw_ways(c, first):
        zc, xc = c // xs, c % xs
        same_x, same_z = xc == x, zc == z
        along_z = same_x | first
        along_x = same_z | jnp.logical_not(first)
        return [
            (0, (z + 1 < zs) & (zc <= z) & along_z),
            (1, (z >= 1) & (zc >= z) & along_z),
            (2, (x + 1 < xs) & (xc <= x) & along_x),
            (3, (x >= 1) & (xc >= x) & along_x),
        ]

    def col_copy(way, c, j, src):
        return remote(way, src, col_raw.at[c, j], col_send.at[way - 4, c], col_recv.at[c, j])

    def raw_step(c, i, src):
        for way, cond in raw_ways(c, i < x_first):
            @pl.when(cond)
            def _(way=way):
                remote(way, src, raw_all.at[c, i], raw_send.at[way, c], raw_recv.at[c, i]).start()
        j = i - half * hch

        @pl.when(is_root & (j >= 0) & (j < hch))
        def _():
            @pl.when(y + 1 < ys)
            def _():
                col_copy(4, c, j, src).start()

            @pl.when(y >= 1)
            def _():
                col_copy(5, c, j, src).start()
            col_copy(6, c, j, src).start()
            pltpu.make_async_copy(src, col_raw.at[c, j], root_sem.at[c, j]).start()

    def col_arrived(c, j):
        pltpu.make_async_copy(col_raw.at[c, j], col_raw.at[c, j], col_recv.at[c, j]).wait()

    keep_raw = pltpu.make_async_copy(raw_own, raw_all.at[col], keep_sem.at[0])
    keep_piv = pltpu.make_async_copy(piv_own, piv_all.at[row, col], keep_sem.at[1])
    keep_raw.start()
    keep_piv.start()

    def own_step(i):
        @pl.when(i < nch)
        def _():
            raw_step(col, i, raw_own.at[i])

    piv_step(y, col, piv_own)
    own_step(0)
    ahead = 1

    @pl.loop(1, span + 1)
    def _(s):
        @pl.loop(0, ys * nc)
        def _(q):
            sy, c = q // nc, q % nc
            dist = jnp.abs(c // xs - z) + jnp.abs(c % xs - x) + jnp.abs(sy - y)

            @pl.when(dist == s)
            def _():
                piv_arrived(sy * 2 + k, c)
                piv_step(sy, c, piv_all.at[sy * 2 + k, c])
        own_step(s)
    ahead = span + 1

    def panel(p, n=1):
        return slice(p * width, (p + n) * width)

    def gather_square():
        @pl.loop(0, ys * nc)
        def _(q):
            piv_arrived((q // nc) * 2 + 1 - k, q % nc)
        keep_piv.wait()

        @pl.loop(0, panels - 1)
        def _(p):
            part = pl.ds(pl.multiple_of(p * width, width), width)
            later = pl.ds(pl.multiple_of((p + 1) * width, width), width)
            rowperm[part, :] = one_hot(icol_ref[later, 2:3] == iota((width, n_row * per_row), 1))

        @pl.loop(0, nc // 2)
        def _(c2):
            block = jnp.concatenate(
                [
                    jnp.concatenate([piv_all[r, c2 * 2 + b, :per_row, :] for b in range(2)], axis=1)
                    for r in range(n_row)
                ],
                axis=0,
            )
            h, l = split(block)
            at_cols = pl.ds(pl.multiple_of(c2 * 2 * wide, 2 * wide), 2 * wide)

            @pl.loop(0, panels - 1)
            def _(p):
                part = pl.ds(pl.multiple_of(p * width, width), width)
                perm = rowperm[part, :]
                a, b = split(mm(perm, h) + mm(perm, l))
                t1h[part, at_cols] = a
                t1l[part, at_cols] = b
        rest = [
            jnp.concatenate(
                [
                    piv_all[r, c, per_row + b * nd : per_row + (b + 1) * nd, :]
                    for r in range(n_row)
                    for b in range(per_row // LANES)
                ],
                axis=1,
            )
            for c in range(nc)
        ]
        h, l = split(jnp.concatenate(rest, axis=0))

        @pl.loop(0, panels - 1)
        def _(p):
            part = pl.ds(pl.multiple_of(p * width, width), width)
            perm = rowperm[part, :]
            a, b = split(mm_t(perm, h) + mm_t(perm, l))
            t1h[part, kraw:] = a
            t1l[part, kraw:] = b

    def dests():
        return jnp.concatenate(
            [piv_all[0, c, per_row + per_row // LANES * nd :, 0:1] for c in range(nc)], axis=0
        ).astype(jnp.int32)

    def square():
        d = dests()

        @pl.loop(0, panels - 1)
        def _(p):
            part = pl.ds(pl.multiple_of(p * width, width), width)
            slot = irow_ref[2:3, part]
            take = one_hot(slot == iota((kraw, width), 0))
            put = one_hot(d == iota((nc * nd, width), 1) + p * width)
            take = jnp.concatenate([take, put], axis=0)

            @pl.loop(0, panels - 1)
            def _(r):
                rows = pl.ds(pl.multiple_of(r * width, width), width)
                h, l = split(mm(t1h[rows, :], take) + mm(t1l[rows, :], take))
                qh[rows, part] = h
                ql[rows, part] = l

    def dot3(a, b, f):
        return f(a[0], b[0]) + f(a[0], b[1]) + f(a[1], b[0])

    def recur():
        nh[...] = jnp.zeros_like(nh)
        nl[...] = jnp.zeros_like(nl)
        for p in range(panels):
            mine = split(linv_ref[p])
            nh[panel(p), panel(p)], nl[panel(p), panel(p)] = mine
            if p == 0:
                continue
            e, until = p - 1, slice(0, p * width)
            for q in range(p, panels):
                rows = panel(q - 1)
                r = dot3((qh[rows, until], ql[rows, until]), (nh[panel(e), until], nl[panel(e), until]), mm_t)
                rd[rows, panel(e)] = pair_scale(r, coef_ref, panel(e))
            b = dot3(mine, split(rd[panel(p - 1), until]), mm)
            out = dot3(split(-b), (nh[until, until], nl[until, until]), mm)
            nh[panel(p), until], nl[panel(p), until] = split(out)

    def spread():
        step = 2 * wide

        @pl.loop(0, kraw // step)
        def _(t):
            part = pl.ds(pl.multiple_of(t * step, step), step)
            take = one_hot(irow_ref[2:3, :] == iota((step, slots), 0) + t * step)
            mh[part, :] = mm_t(take, nh[...]).astype(BF16)
            ml[part, :] = mm_t(take, nl[...]).astype(BF16)
        put = one_hot(dests() == iota((nc * nd, slots), 1))
        mh[kraw:, :] = mm_t(put, nh[...]).astype(BF16)
        ml[kraw:, :] = mm_t(put, nl[...]).astype(BF16)

    def chunk_parts(ref, i):
        a = jnp.concatenate([ref[c, i, :ch, :] for c in range(nc)], axis=1)
        d = jnp.concatenate(
            [
                jnp.concatenate([ref[c, i, ch + b * nd : ch + (b + 1) * nd, :] for b in range(ch // LANES)], axis=1)
                for c in range(nc)
            ],
            axis=0,
        )
        return split(jnp.concatenate([a, d.T], axis=1))

    def scaled_tile(parts, part):
        return mm(parts[0], mh[:, part]) + mm(parts[0], ml[:, part]) + mm(parts[1], mh[:, part])

    def cols_copy(i):
        rows = pl.ds(pl.multiple_of(i * ch, ch), ch)
        return pltpu.make_async_copy(stage.at[i % 2], cols_out.at[rows, :], out_sem.at[i % 2])

    def eliminate(i):
        @pl.when(i >= 2)
        def _():
            cols_copy(i - 2).wait()
        parts = chunk_parts(raw_all, i)

        @pl.loop(0, panels)
        def _(p):
            part = pl.ds(pl.multiple_of(p * width, width), width)
            stage[i % 2, :, part] = pair_scale(scaled_tile(parts, part), coef_ref, part)
        cols_copy(i).start()

    def side_copies(j):
        cols = pl.ds(pl.multiple_of(j * ch, ch), ch)
        return (
            pltpu.make_async_copy(stage_h.at[j % 2], hi_out.at[:, cols], hi_sem.at[j % 2]),
            pltpu.make_async_copy(stage_l.at[j % 2], lo_out.at[:, cols], lo_sem.at[j % 2]),
        )

    def eliminate_side(j):
        @pl.when(k != root_k)
        def _():
            @pl.loop(0, nc)
            def _(c):
                col_arrived(c, j)

        @pl.when(is_root)
        def _():
            @pl.loop(0, nc)
            def _(c):
                pltpu.make_async_copy(col_raw.at[c, j], col_raw.at[c, j], root_sem.at[c, j]).wait()

        @pl.when(j >= 2)
        def _():
            for copy in side_copies(j - 2):
                copy.wait()
        parts = chunk_parts(col_raw, j)

        @pl.loop(0, panels)
        def _(p):
            part = pl.ds(pl.multiple_of(p * width, width), width)
            stage_h[j % 2, part, :], stage_l[j % 2, part, :] = split(scaled_tile(parts, part).T)
        for copy in side_copies(j):
            copy.start()

    first = max(reach - 1, 3)
    side_lag = reach - 1 + ys
    work = [gather_square, square, recur]

    @pl.loop(0, nch + max(first, side_lag))
    def _(s):
        own_step(s + ahead)

        @pl.loop(0, nc)
        def _(c):
            dist = jnp.abs(c // xs - z) + jnp.abs(c % xs - x)
            i = s - (dist - 1)

            @pl.when((dist >= 1) & (i >= 0) & (i < nch))
            def _():
                pltpu.make_async_copy(raw_all.at[c, i], raw_all.at[c, i], raw_recv.at[c, i]).wait()
                raw_step(c, i, raw_all.at[c, i])

        @pl.when(at_root_core & (y != root_y))
        def _():
            @pl.loop(0, nc)
            def _(c):
                dist = jnp.abs(c // xs - z) + jnp.abs(c % xs - x)
                j = s - (jnp.maximum(dist, 1) - 1) - jnp.abs(y - root_y) - half * hch

                @pl.when((j >= 0) & (j < hch))
                def _():
                    col_arrived(c, j)
                    src = col_raw.at[c, j]

                    @pl.when((y > root_y) & (y + 1 < ys))
                    def _():
                        col_copy(4, c, j, src).start()

                    @pl.when((y < root_y) & (y >= 1))
                    def _():
                        col_copy(5, c, j, src).start()
                    col_copy(6, c, j, src).start()

        for n, piece in enumerate(work):
            pl.when(s == n)(piece)

        @pl.when(s == len(work) - 1)
        def _():
            spread()
            keep_raw.wait()

        i = s - first

        @pl.when((i >= 0) & (i < nch))
        def _():
            eliminate(i)
        j = s - side_lag - half * hch

        @pl.when((j >= 0) & (j < hch))
        def _():
            eliminate_side(j)

    for i in range(max(nch - 2, 0), nch):
        cols_copy(i).wait()
    for j in range(max(hch - 2, 0), hch):
        for copy in side_copies(j):
            copy.wait()

    @pl.loop(0, ys * nc)
    def _(q):
        sy, c = q // nc, q % nc
        for way, cond in piv_ways(sy, c):
            @pl.when(cond)
            def _(way=way):
                piv_copy(way, sy, c, piv_own).wait_send()
        piv_copy(6, sy, c, piv_own).wait_send()

    def sent(ref, sem):
        pltpu.make_async_copy(ref, ref, sem).wait()

    @pl.loop(0, nc)
    def _(c):
        for (way, late), (_, early) in zip(raw_ways(c, False), raw_ways(c, True)):
            sem = raw_send.at[way, c]

            @pl.when(late & early)
            def _(sem=sem):
                sent(raw_all.at[c], sem)

            if x_first:
                @pl.when(jnp.logical_not(late) & early)
                def _(sem=sem):
                    sent(raw_all.at[c, pl.ds(0, x_first)], sem)

                @pl.when(late & jnp.logical_not(early))
                def _(sem=sem):
                    sent(raw_all.at[c, pl.ds(x_first, nch - x_first)], sem)
            else:
                @pl.when(late & jnp.logical_not(early))
                def _(sem=sem):
                    sent(raw_all.at[c], sem)

        @pl.when(is_root | (at_root_core & (y > root_y)))
        def _():
            @pl.when(y + 1 < ys)
            def _():
                sent(col_raw.at[c], col_send.at[0, c])

        @pl.when(is_root | (at_root_core & (y < root_y)))
        def _():
            @pl.when(y >= 1)
            def _():
                sent(col_raw.at[c], col_send.at[1, c])

        @pl.when(at_root_core)
        def _():
            sent(col_raw.at[c], col_send.at[2, c])


def pair_scale(scaled, coef_ref, part):
    width = scaled.shape[1]
    return (
        scaled * coef_ref[0:1, part]
        + pltpu.roll(scaled, width - 1, 1) * coef_ref[1:2, part]
        + pltpu.roll(scaled, 1, 1) * coef_ref[2:3, part]
    )


def gather(raw, piv, linv, coef, irow, icol, cols, per_row, nd):
    n_col = lax.axis_size("col")
    n_row = lax.axis_size("row")
    nch, high, wide = raw.shape
    panels, width, _ = linv.shape
    slots = panels * width
    rows = nch * CHUNK
    halves = rows // cols
    ys = n_row // 2
    xs = ys if n_col % ys == 0 else 1
    zs = n_col // xs
    hch = nch // halves
    x_first = nch // 6
    kall = n_col * (wide + nd)
    early = slots - width
    vmem = pl.BlockSpec(memory_space=pltpu.VMEM)
    hbm = pl.BlockSpec(memory_space=pl.ANY)
    dma = pltpu.SemaphoreType.DMA
    return pl.pallas_call(
        functools.partial(gather_kernel, (zs, xs, ys, halves, per_row, nd, x_first)),
        out_shape=(
            jax.ShapeDtypeStruct((rows, slots), F32),
            jax.ShapeDtypeStruct((slots, cols), BF16),
            jax.ShapeDtypeStruct((slots, cols), BF16),
        ),
        in_specs=[vmem] * 6,
        out_specs=(hbm, hbm, hbm),
        scratch_shapes=[
            pltpu.VMEM((n_col, nch, high, wide), F32),
            pltpu.VMEM((n_col, hch, high, wide), F32),
            pltpu.VMEM((n_row, n_col) + piv.shape, F32),
            pltpu.VMEM((early, slots), BF16),
            pltpu.VMEM((early, kall), BF16),
            pltpu.VMEM((early, kall), BF16),
            pltpu.VMEM((early, early), BF16),
            pltpu.VMEM((early, early), BF16),
            pltpu.VMEM((slots, slots), BF16),
            pltpu.VMEM((slots, slots), BF16),
            pltpu.VMEM((early, early), F32),
            pltpu.VMEM((kall, slots), BF16),
            pltpu.VMEM((kall, slots), BF16),
            pltpu.VMEM((2, CHUNK, slots), F32),
            pltpu.VMEM((2, slots, CHUNK), BF16),
            pltpu.VMEM((2, slots, CHUNK), BF16),
            dma((2,)),
            dma((n_col, hch)),
            dma((n_col, nch)),
            dma((4, n_col)),
            dma((n_col, hch)),
            dma((3, n_col)),
            dma((n_row, n_col)),
            dma((7, ys * n_col)),
            dma((2,)),
            dma((2,)),
            dma((2,)),
        ],
        compiler_params=pltpu.CompilerParams(
            collective_id=0, has_side_effects=True, vmem_limit_bytes=VMEM_LIMIT
        ),
    )(raw, piv, linv, coef, irow, icol)


def trailing_kernel(tile, c_ref, hi_ref, lo_ref, front_ref, rkeep_ref, ckeep_ref, out_ref, factor_ref):
    cols = hi_ref.shape[1]
    columns = c_ref[...]
    factor_ref[...] = columns
    hi, lo = split(columns)
    rkeep = rkeep_ref[...] > 0.0

    @pl.loop(0, cols // tile)
    def _(i):
        part = pl.ds(pl.multiple_of(i * tile, tile), tile)
        bh, bl = hi_ref[:, part], lo_ref[:, part]
        acc = mm(hi, bh) + mm(hi, bl) + mm(lo, bh)
        out_ref[:, part] = jnp.where(rkeep & (ckeep_ref[:, part] > 0.0), front_ref[:, part] - acc, 0.0)


def update(columns, side_hi, side_lo, front, row_keep, col_keep):
    rows, cols = front.shape
    slots = columns.shape[1]
    tile = 256
    return pl.pallas_call(
        functools.partial(trailing_kernel, tile),
        grid=(rows // tile,),
        in_specs=[
            pl.BlockSpec((tile, slots), lambda i: (i, 0)),
            pl.BlockSpec((slots, cols), lambda i: (0, 0)),
            pl.BlockSpec((slots, cols), lambda i: (0, 0)),
            pl.BlockSpec((tile, cols), lambda i: (i, 0)),
            pl.BlockSpec((tile, 1), lambda i: (i, 0)),
            pl.BlockSpec((1, cols), lambda i: (0, 0)),
        ],
        out_specs=(
            pl.BlockSpec((tile, cols), lambda i: (i, 0)),
            pl.BlockSpec((tile, slots), lambda i: (i, 0)),
        ),
        out_shape=(
            jax.ShapeDtypeStruct((rows, cols), F32),
            jax.ShapeDtypeStruct((rows, slots), F32),
        ),
        compiler_params=pltpu.CompilerParams(dimension_semantics=("arbitrary",), vmem_limit_bytes=VMEM_LIMIT),
    )(columns, side_hi, side_lo, front, row_keep, col_keep)


def body(front, delayed, dest, pivots, pair_flags, linv, dinv_diag, dinv_off):
    n_col = lax.axis_size("col")
    n_row = lax.axis_size("row")
    rows, cols = front.shape
    row_id = lax.axis_index("row")
    col_id = lax.axis_index("col")
    row_start = row_id * rows
    col_start = col_id * cols
    panels, width, _ = linv.shape
    slots = pivots.shape[0]
    per_col = slots // n_col
    per_row = slots // n_row
    wide = (per_col + LANES - 1) // LANES * LANES
    nd = delayed.shape[0]
    slot_ids = jnp.arange(slots, dtype=jnp.int32)

    col_owner = pivots // cols
    row_owner = pivots // rows
    before = slot_ids[None, :] < slot_ids[:, None]
    col_rank = jnp.sum((before & (col_owner[:, None] == col_owner[None, :])).astype(jnp.int32), axis=1)
    row_rank = jnp.sum((before & (row_owner[:, None] == row_owner[None, :])).astype(jnp.int32), axis=1)
    col_pos = col_owner * wide + col_rank
    row_pos = row_owner * per_row + row_rank
    pad = jnp.zeros_like(pivots)
    irow = jnp.stack([pivots - col_start, row_pos - row_id * per_row, col_pos] + [pad] * 5)
    icol = jnp.stack([pivots - row_start, col_pos - col_id * wide, row_pos] + [pad] * 5, axis=1)

    in_panel = slot_ids % width
    coupled = pair_flags.astype(F32) * dinv_off
    zero = jnp.zeros_like(dinv_diag)
    coef = jnp.stack(
        [dinv_diag, jnp.where(in_panel == width - 1, 0.0, coupled), jnp.where(in_panel == 0, 0.0, jnp.roll(coupled, 1))]
        + [zero] * 5
    )
    row_in = jnp.any((row_start + jnp.arange(rows))[:, None] == pivots[None, :], axis=1)
    col_in = jnp.any((col_start + jnp.arange(cols))[:, None] == pivots[None, :], axis=1)
    row_keep = jnp.where(row_in, 0.0, 1.0)[:, None]
    col_keep = jnp.where(col_in, 0.0, 1.0)[None, :]

    dest_wide = jnp.broadcast_to(dest.astype(F32)[:, None], (nd, wide))
    raw, piv = pick_columns(front, delayed, dest_wide, irow, icol, wide, per_row)
    columns, side_hi, side_lo = gather(raw, piv, linv, coef, irow, icol, cols, per_row, nd)
    trailing, factor = update(columns, side_hi, side_lo, front, row_keep, col_keep)
    return (trailing, factor)


def solution(mesh):
    return jax.shard_map(
        body,
        mesh=mesh,
        in_specs=(P("row", "col"), P("col", "row"), P("col"), P(), P(), P(), P(), P()),
        out_specs=(P("row", "col"), P("row", None)),
        check_vma=False,
    )
```

time: 423 us -> 293 us (0.69)
  the two profiles are of different devices: /device:TPU:5 before, /device:TPU:7 now
where the time goes in v1:
time: 293 us; the launch traced here: 290 us
  Pallas kernels  272 us (93%)
  other arithmetic  10.2 us (3%)
  local copies, waits for them, and re-layouts  6.56 us (2%)
    pallas_call x1, Pallas kernels, gather(): pl.pallas_call(functools.partial(gather_kernel, (zs, xs, ys, halves, per_...  201 us
    pallas_call x1, Pallas kernels, update(): pl.pallas_call(functools.partial(trailing_kernel, tile), grid=(rows // ti...  51.4 us
    pallas_call x1, Pallas kernels, pick_columns(): pl.pallas_call(pick_kernel, grid=(n,), in_specs=[pl.BlockSpec((CHUNK, col...  19.6 us

profile of v1, /device:TPU:7, one launch (start us, length us, event | category | flops | bytes accessed | tf_op | source)
XLA Modules:
  0.0 289.6 jit_solution(17905996417959108698)
XLA Ops:
  0.6 0.7 convert_element_type.12
  1.3 0.7 broadcast_in_dim.25.dest_ref
  2.0 1.7 compare_reduce_fusion.1
  3.6 0.6 select_n.75.ckeep_ref
  4.2 0.7 fusion.8
  5.0 0.6 slice.8
  5.5 0.7 compare_select_fusion
  6.3 0.7 add_select_fusion.1
  7.0 2.3 convert_reduce_fusion
  9.3 2.7 compare_reduce_fusion
  12.0 0.7 broadcast_subtract_fusion
  12.8 0.7 stack.47.irow_ref
  13.5 1.3 stack.56.coef_ref
  14.8 1.0 copy.17.icol_ref
  15.8 1.7 copy.19.rkeep_ref
  17.5 19.6 %shard_map.95 = (f32[12,272,128]{2,1,0:T(8,128)}, f32[280,128]{1,0:T(8,128)}) custom-call(f32[3072,1536]{1,0:T(8,128)} %front_ref.3, f32[8,3072]{1,0:T(8,128)} %delayed_ref.1, f32[8,128]{1,0:T(8,128)} %broadcast_in_dim.25.dest_ref, s32[8,1024]{1,0:T(8,128)} %stack.47.irow_ref, s32[1024,8]{1,0:T(8,128)} %copy.17.icol_ref), custom_call_target="tpu_custom_call" | custom-call | tf_op jit(solution)/shard_map/pallas_call | solution.py:90
  37.1 201.1 %shard_map.96 = (f32[3072,1024]{1,0:T(8,128)}, bf16[1024,1536]{1,0:T(8,128)(2,1)}, bf16[1024,1536]{1,0:T(8,128)(2,1)}) custom-call(f32[12,272,128]{2,1,0:T(8,128)} %get-tuple-element.7.raw_own, f32[280,128]{1,0:T(8,128)} %get-tuple-element.8.piv_own, f32[4,256,256]{2,1,0:T(8,128)} %linv_ref.1, f32[8,1024]{1,0:T(8,128)} %stack.56.coef_ref, ...), custom_call_target="tpu_custom_call" | custom-call | tf_op jit(solution)/shard_map/pallas_call | solution.py:584
  238.2 51.4 %shard_map.97 = (f32[3072,1536]{1,0:T(8,128)}, f32[3072,1024]{1,0:T(8,128)}) custom-call(f32[3072,1024]{1,0:T(8,128)} %get-tuple-element.9.c_ref, bf16[1024,1536]{1,0:T(8,128)(2,1)} %get-tuple-element.10.hi_ref, bf16[1024,1536]{1,0:T(8,128)(2,1)} %get-tuple-element.11.lo_ref, f32[3072,1536]{1,0:T(8,128)} %front_ref.3, f32[3072,1]{1,0:T(8,128)} %copy.19.rkeep_ref, ...), custom_call_target="tpu_custom_call" | custom-call | tf_op jit(solution)/shard_map/pallas_call | solution.py:647
  (11 shorter events, 0.1 us)

commit v2 on v1

--- a/solution.py
+++ b/solution.py
@@ -12,6 +12,8 @@
 F32 = jnp.float32
 BF16 = jnp.bfloat16
 CHUNK = 256
+COMM = 256
+WIDE = 4
 LANES = 128
 
 
@@ -36,37 +38,87 @@
     return jnp.where(mask, 1.0, 0.0).astype(BF16)
 
 
-def pick_kernel(front_ref, delayed_ref, dest_ref, irow_ref, icol_ref, raw_ref, piv_ref, g_ref, rowsel_ref, acc_ref, dacc_ref):
+def owner_of(ids, block, n):
+    total = jnp.zeros(ids.shape, F32)
+    for c in range(1, n):
+        total += jnp.where(ids >= c * block, 1.0, 0.0)
+    return total
+
+
+def rank_of(owner_row, owner_col):
+    slots = owner_row.shape[1]
+    total = jnp.zeros((1, slots), F32)
+    for t in range(slots // CHUNK):
+        here = slice(t * CHUNK, (t + 1) * CHUNK)
+        before = iota((CHUNK, slots), 0) + t * CHUNK < iota((CHUNK, slots), 1)
+        same = owner_col[here, :] == owner_row
+        total += jnp.sum(jnp.where(before & same, 1.0, 0.0), axis=0, keepdims=True)
+    return total
+
+
+def turned(row):
+    return jnp.broadcast_to(row, (8, row.shape[1])).T[:, 0:1]
+
+
+def pick_kernel(
+    dims, front_ref, delayed_ref, dest_ref, ids_ref, dinv_ref,
+    raw_ref, piv_ref, irow_ref, icol_ref, coef_ref, g_ref, want_ref, acc_ref, dacc_ref,
+):
+    n_row, n_col, rows, width, per_col = dims
     i = pl.program_id(0)
-    slots = irow_ref.shape[1]
+    slots = ids_ref.shape[1]
     cols, wide = g_ref.shape
-    per_row = rowsel_ref.shape[0]
+    per_row = want_ref.shape[0]
     nd = delayed_ref.shape[0]
-    ch = front_ref.shape[0]
+    tile = front_ref.shape[0]
+    high = raw_ref.shape[1]
+    ch = tile // raw_ref.shape[0]
+    row_id, col_id = lax.axis_index("row"), lax.axis_index("col")
 
     @pl.when(i == 0)
     def _():
-        y = one_hot(icol_ref[:, 1:2] == iota((slots, wide), 1))
-
-        @pl.loop(0, cols // CHUNK)
-        def _(t):
-            part = pl.ds(pl.multiple_of(t * CHUNK, CHUNK), CHUNK)
-            x = one_hot(irow_ref[0:1, :] == iota((CHUNK, slots), 0) + t * CHUNK)
-            g_ref[part, :] = mm(x, y).astype(BF16)
-
-        rowsel_ref[...] = one_hot(irow_ref[1:2, :] == iota((per_row, slots), 0))
+        piv = ids_ref[0:1, :].astype(F32)
+        col_owner = owner_of(piv, cols, n_col)
+        row_owner = owner_of(piv, rows, n_row)
+        col_pos = col_owner * wide + rank_of(col_owner, turned(col_owner))
+        row_pos = row_owner * per_row + rank_of(row_owner, turned(row_owner))
+        piv_col = turned(piv)
+        row_pos_col, col_pos_col = turned(row_pos), turned(col_pos)
+        irow_ref[...] = jnp.zeros_like(irow_ref)
+        irow_ref[0:1, :] = piv
+        irow_ref[1:2, :] = col_pos
+        icol_ref[...] = jnp.zeros_like(icol_ref)
+        icol_ref[:, 0:1] = row_pos_col
+        icol_ref[:, 1:2] = piv_col
+
+        mine = col_pos_col - (col_id * wide).astype(F32) == iota((slots, wide), 1).astype(F32)
+        want_col = jnp.sum(jnp.where(mine, piv_col - (col_id * cols).astype(F32), 0.0), axis=0, keepdims=True)
+        real = iota((1, wide), 1) < per_col
+        want_col = jnp.where(real, want_col, -1.0)
+        g_ref[...] = one_hot(iota((cols, wide), 0).astype(F32) == want_col)
+        mine = row_pos - (row_id * per_row).astype(F32) == iota((per_row, slots), 0).astype(F32)
+        want_ref[...] = jnp.sum(jnp.where(mine, piv - (row_id * rows).astype(F32), 0.0), axis=1, keepdims=True)
+
+        slot = iota((1, slots), 1) % width
+        coupled = ids_ref[1:2, :].astype(F32) * dinv_ref[1:2, :]
+        coef_ref[...] = jnp.zeros_like(coef_ref)
+        coef_ref[0:1, :] = dinv_ref[0:1, :]
+        coef_ref[1:2, :] = jnp.where(slot == width - 1, 0.0, coupled)
+        coef_ref[2:3, :] = jnp.where(slot == 0, 0.0, pltpu.roll(jnp.broadcast_to(coupled, (8, slots)), 1, 1)[0:1, :])
         acc_ref[...] = jnp.zeros_like(acc_ref)
         dacc_ref[...] = jnp.zeros_like(dacc_ref)
 
     hi, lo = split(front_ref[...])
     g = g_ref[...]
     raw = mm(hi, g) + mm(lo, g)
-    raw_ref[0, :ch, :] = raw
-    for b in range(ch // LANES):
-        raw_ref[0, ch + b * nd : ch + (b + 1) * nd, :] = delayed_ref[:, b * LANES : (b + 1) * LANES]
-
-    here = one_hot(icol_ref[:, 0:1] == iota((slots, ch), 1) + i * ch)
-    sel = mm(rowsel_ref[...], here).astype(BF16)
+    for b in range(raw_ref.shape[0]):
+        raw_ref[b, :ch, :] = raw[b * ch : (b + 1) * ch, :]
+        for t in range(ch // LANES):
+            at = b * ch + t * LANES
+            raw_ref[b, ch + t * nd : ch + (t + 1) * nd, :] = delayed_ref[:, at : at + LANES]
+
+    start = row_tile(i, rows // tile, rows // cols) * tile
+    sel = one_hot(want_ref[...].astype(jnp.int32) - start == iota((per_row, tile), 1))
     rh, rl = split(raw)
     acc_ref[...] += mm(sel, rh) + mm(sel, rl)
     dh, dl = split(delayed_ref[...])
@@ -77,51 +129,68 @@
         piv_ref[:per_row, :] = acc_ref[...]
         for b in range(per_row // LANES):
             piv_ref[per_row + b * nd : per_row + (b + 1) * nd, :] = dacc_ref[:, b * LANES : (b + 1) * LANES]
-        piv_ref[per_row + per_row // LANES * nd :, :] = dest_ref[...]
-
-
-def pick_columns(front, delayed, dest, irow, icol, wide, per_row):
+        diagonal = iota((nd, nd), 0) == iota((nd, nd), 1)
+        dest = jnp.sum(jnp.where(diagonal, dest_ref[...].astype(F32), 0.0), axis=1, keepdims=True)
+        piv_ref[per_row + per_row // LANES * nd :, :] = jnp.broadcast_to(dest, (nd, wide))
+
+
+def row_tile(i, tiles, halves):
+    return i % halves * (tiles // halves) + i // halves
+
+
+def pick_columns(front, delayed, dest, ids, dinv, n_row, n_col, wide, width):
     rows, cols = front.shape
     nd = delayed.shape[0]
-    slots = irow.shape[1]
-    n = rows // CHUNK
-    high = CHUNK + nd * (CHUNK // LANES)
+    slots = ids.shape[1]
+    per_row = slots // n_row
+    halves = rows // cols
+    tile = CHUNK
+    n = rows // tile
+    sub = tile // COMM
+    high = COMM + nd * (COMM // LANES)
     piv_high = per_row + nd * (per_row // LANES) + nd
+    dims = (n_row, n_col, rows, width, slots // n_col)
     return pl.pallas_call(
-        pick_kernel,
+        functools.partial(pick_kernel, dims),
         grid=(n,),
         in_specs=[
-            pl.BlockSpec((CHUNK, cols), lambda i: (i, 0)),
-            pl.BlockSpec((nd, CHUNK), lambda i: (0, i)),
-            pl.BlockSpec((nd, wide), lambda i: (0, 0)),
+            pl.BlockSpec((tile, cols), lambda i: (row_tile(i, n, halves), 0)),
+            pl.BlockSpec((nd, tile), lambda i: (0, row_tile(i, n, halves))),
+            pl.BlockSpec((1, nd), lambda i: (0, 0)),
+            pl.BlockSpec((2, slots), lambda i: (0, 0)),
+            pl.BlockSpec((2, slots), lambda i: (0, 0)),
+        ],
+        out_specs=(
+            pl.BlockSpec((sub, high, wide), lambda i: (i, 0, 0)),
+            pl.BlockSpec((piv_high, wide), lambda i: (0, 0)),
             pl.BlockSpec((8, slots), lambda i: (0, 0)),
             pl.BlockSpec((slots, 8), lambda i: (0, 0)),
-        ],
-        out_specs=(
-            pl.BlockSpec((1, high, wide), lambda i: (i, 0, 0)),
-            pl.BlockSpec((piv_high, wide), lambda i: (0, 0)),
+            pl.BlockSpec((8, slots), lambda i: (0, 0)),
         ),
         out_shape=(
-            jax.ShapeDtypeStruct((n, high, wide), F32),
+            jax.ShapeDtypeStruct((n * sub, high, wide), F32),
             jax.ShapeDtypeStruct((piv_high, wide), F32),
+            jax.ShapeDtypeStruct((8, slots), F32),
+            jax.ShapeDtypeStruct((slots, 8), F32),
+            jax.ShapeDtypeStruct((8, slots), F32),
         ),
         scratch_shapes=[
             pltpu.VMEM((cols, wide), BF16),
-            pltpu.VMEM((per_row, slots), BF16),
+            pltpu.VMEM((per_row, 1), F32),
             pltpu.VMEM((per_row, wide), F32),
             pltpu.VMEM((nd, per_row), F32),
         ],
         compiler_params=pltpu.CompilerParams(dimension_semantics=("arbitrary",), vmem_limit_bytes=VMEM_LIMIT),
-    )(front, delayed, dest, irow, icol)
+    )(front, delayed, dest, ids, dinv)
 
 
 def gather_kernel(
     dims, raw_own, piv_own, linv_ref, coef_ref, irow_ref, icol_ref,
-    cols_out, hi_out, lo_out,
+    cols_out, hi_out, lo_out, rkeep_ref, ckeep_ref,
     raw_all, col_raw, piv_all, rowperm, t1h, t1l, qh, ql, nh, nl, rd, mh, ml, stage, stage_h, stage_l,
     keep_sem, root_sem, raw_recv, raw_send, col_recv, col_send, piv_recv, piv_send, out_sem, hi_sem, lo_sem,
 ):
-    zs, xs, ys, halves, per_row, nd, x_first = dims
+    zs, xs, ys, halves, per_row, nd, x_rows = dims
     nc, n_row = zs * xs, ys * 2
     nch = raw_own.shape[0]
     high = raw_own.shape[1]
@@ -129,9 +198,10 @@
     panels, width, _ = linv_ref.shape
     slots = panels * width
     wide = raw_own.shape[2]
-    ch = CHUNK
+    ch = COMM
+    sub = CHUNK // COMM
+    z_part, x_part = pl.ds(0, high - x_rows), pl.ds(high - x_rows, x_rows)
     kraw = nc * wide
-    kall = mh.shape[0]
     row, col = lax.axis_index("row"), lax.axis_index("col")
     y, k = row // 2, row % 2
     z, x = col // xs, col % xs
@@ -200,29 +270,51 @@
                 piv_copy(way, sy, c, src).start()
         piv_copy(6, sy, c, src).start()
 
-    def raw_ways(c, first):
+    def raw_ways(c):
         zc, xc = c // xs, c % xs
         same_x, same_z = xc == x, zc == z
-        along_z = same_x | first
-        along_x = same_z | jnp.logical_not(first)
         return [
-            (0, (z + 1 < zs) & (zc <= z) & along_z),
-            (1, (z >= 1) & (zc >= z) & along_z),
-            (2, (x + 1 < xs) & (xc <= x) & along_x),
-            (3, (x >= 1) & (xc >= x) & along_x),
+            (0, (z + 1 < zs) & (zc <= z), same_x, x_part),
+            (1, (z >= 1) & (zc >= z), same_x, x_part),
+            (2, (x + 1 < xs) & (xc <= x), same_z, z_part),
+            (3, (x >= 1) & (xc >= x), same_z, z_part),
         ]
+
+    def side_of(i):
+        e = i // sub
+        return e // halves * sub + i % sub, (i >= 0) & (i < nch) & (e % halves == half)
+
+    def raw_arrived(c, i):
+        line = (c // xs == z) | (c % xs == x)
+        whole = raw_all.at[c, i]
+
+        @pl.when(line)
+        def _():
+            pltpu.make_async_copy(whole, whole, raw_recv.at[c, i, 0]).wait()
+
+        @pl.when(jnp.logical_not(line))
+        def _():
+            for n, part in enumerate((z_part, x_part)):
+                ref = raw_all.at[c, i, part]
+                pltpu.make_async_copy(ref, ref, raw_recv.at[c, i, n]).wait()
 
     def col_copy(way, c, j, src):
         return remote(way, src, col_raw.at[c, j], col_send.at[way - 4, c], col_recv.at[c, j])
 
     def raw_step(c, i, src):
-        for way, cond in raw_ways(c, i < x_first):
-            @pl.when(cond)
+        for way, cond, line, part in raw_ways(c):
+            @pl.when(cond & line)
             def _(way=way):
-                remote(way, src, raw_all.at[c, i], raw_send.at[way, c], raw_recv.at[c, i]).start()
-        j = i - half * hch
-
-        @pl.when(is_root & (j >= 0) & (j < hch))
+                remote(way, src, raw_all.at[c, i], raw_send.at[way, c], raw_recv.at[c, i, 0]).start()
+
+            @pl.when(cond & jnp.logical_not(line))
+            def _(way=way, part=part):
+                remote(
+                    way, src.at[part], raw_all.at[c, i, part],
+                    raw_send.at[way, c], raw_recv.at[c, i, 1 if way < 2 else 0]).start()
+        j, mine = side_of(i)
+
+        @pl.when(is_root & mine)
         def _():
             @pl.when(y + 1 < ys)
             def _():
@@ -268,6 +360,22 @@
     def panel(p, n=1):
         return slice(p * width, (p + n) * width)
 
+    def masks():
+        n = ckeep_ref.shape[1] // CHUNK
+
+        @pl.loop(0, n)
+        def _(t):
+            ids = iota((slots, CHUNK), 1) + t * CHUNK + col * (n * CHUNK)
+            hit = jnp.where(icol_ref[:, 1:2].astype(jnp.int32) == ids, 1.0, 0.0)
+            ckeep_ref[:, pl.ds(pl.multiple_of(t * CHUNK, CHUNK), CHUNK)] = 1.0 - jnp.max(hit, axis=0, keepdims=True)
+        n = rkeep_ref.shape[0] // CHUNK
+
+        @pl.loop(0, n)
+        def _(t):
+            ids = iota((CHUNK, slots), 0) + t * CHUNK + row * (n * CHUNK)
+            hit = jnp.where(irow_ref[0:1, :].astype(jnp.int32) == ids, 1.0, 0.0)
+            rkeep_ref[pl.ds(pl.multiple_of(t * CHUNK, CHUNK), CHUNK), :] = 1.0 - jnp.max(hit, axis=1, keepdims=True)
+
     def gather_square():
         @pl.loop(0, ys * nc)
         def _(q):
@@ -278,7 +386,7 @@
         def _(p):
             part = pl.ds(pl.multiple_of(p * width, width), width)
             later = pl.ds(pl.multiple_of((p + 1) * width, width), width)
-            rowperm[part, :] = one_hot(icol_ref[later, 2:3] == iota((width, n_row * per_row), 1))
+            rowperm[part, :] = one_hot(icol_ref[later, 0:1].astype(jnp.int32) == iota((width, n_row * per_row), 1))
 
         @pl.loop(0, nc // 2)
         def _(c2):
@@ -331,7 +439,7 @@
         @pl.loop(0, panels - 1)
         def _(p):
             part = pl.ds(pl.multiple_of(p * width, width), width)
-            slot = irow_ref[2:3, part]
+            slot = irow_ref[1:2, part].astype(jnp.int32)
             take = one_hot(slot == iota((kraw, width), 0))
             put = one_hot(d == iota((nc * nd, width), 1) + p * width)
             take = jnp.concatenate([take, put], axis=0)
@@ -369,74 +477,78 @@
         @pl.loop(0, kraw // step)
         def _(t):
             part = pl.ds(pl.multiple_of(t * step, step), step)
-            take = one_hot(irow_ref[2:3, :] == iota((step, slots), 0) + t * step)
+            take = one_hot(irow_ref[1:2, :].astype(jnp.int32) == iota((step, slots), 0) + t * step)
             mh[part, :] = mm_t(take, nh[...]).astype(BF16)
             ml[part, :] = mm_t(take, nl[...]).astype(BF16)
         put = one_hot(dests() == iota((nc * nd, slots), 1))
-        mh[kraw:, :] = mm_t(put, nh[...]).astype(BF16)
-        ml[kraw:, :] = mm_t(put, nl[...]).astype(BF16)
-
-    def chunk_parts(ref, i):
-        a = jnp.concatenate([ref[c, i, :ch, :] for c in range(nc)], axis=1)
+        h = mm_t(put, nh[...]).astype(BF16)
+        mh[kraw:, :] = jnp.concatenate([h, mm_t(put, nl[...]).astype(BF16), h], axis=0)
+
+    def chunk_parts(ref, e):
+        blocks = [e * sub + b for b in range(sub)]
+        a = jnp.concatenate(
+            [jnp.concatenate([ref[c, i, :ch, :] for c in range(nc)], axis=1) for i in blocks], axis=0)
         d = jnp.concatenate(
             [
-                jnp.concatenate([ref[c, i, ch + b * nd : ch + (b + 1) * nd, :] for b in range(ch // LANES)], axis=1)
+                jnp.concatenate(
+                    [ref[c, i, ch + b * nd : ch + (b + 1) * nd, :] for i in blocks for b in range(ch // LANES)], axis=1)
                 for c in range(nc)
             ],
             axis=0,
         )
-        return split(jnp.concatenate([a, d.T], axis=1))
+        dh, dl = split(d.T)
+        ah, al = split(a)
+        return jnp.concatenate([ah, dh, dh, dl], axis=1), ah, al
 
     def scaled_tile(parts, part):
-        return mm(parts[0], mh[:, part]) + mm(parts[0], ml[:, part]) + mm(parts[1], mh[:, part])
-
-    def cols_copy(i):
-        rows = pl.ds(pl.multiple_of(i * ch, ch), ch)
-        return pltpu.make_async_copy(stage.at[i % 2], cols_out.at[rows, :], out_sem.at[i % 2])
-
-    def eliminate(i):
-        @pl.when(i >= 2)
-        def _():
-            cols_copy(i - 2).wait()
-        parts = chunk_parts(raw_all, i)
-
-        @pl.loop(0, panels)
-        def _(p):
-            part = pl.ds(pl.multiple_of(p * width, width), width)
-            stage[i % 2, :, part] = pair_scale(scaled_tile(parts, part), coef_ref, part)
-        cols_copy(i).start()
-
-    def side_copies(j):
-        cols = pl.ds(pl.multiple_of(j * ch, ch), ch)
+        return mm(parts[0], mh[:, part]) + mm(parts[1], ml[:, part]) + mm(parts[2], mh[:kraw, part])
+
+    def cols_copy(e):
+        rows = pl.ds(pl.multiple_of(row_tile(e, nch // sub, halves) * CHUNK, CHUNK), CHUNK)
+        return pltpu.make_async_copy(stage.at[e % 2], cols_out.at[rows, :], out_sem.at[e % 2])
+
+    def eliminate(e):
+        @pl.when(e >= 2)
+        def _():
+            cols_copy(e - 2).wait()
+        parts = chunk_parts(raw_all, e)
+        for p in range(0, panels, WIDE):
+            scaled = scaled_tile(parts, panel(p, WIDE))
+            stage[e % 2, :, panel(p, WIDE)] = pair_scale(scaled, coef_ref, panel(p, WIDE))
+        cols_copy(e).start()
+
+    def side_copies(e):
+        cols = pl.ds(pl.multiple_of(e * CHUNK, CHUNK), CHUNK)
         return (
-            pltpu.make_async_copy(stage_h.at[j % 2], hi_out.at[:, cols], hi_sem.at[j % 2]),
-            pltpu.make_async_copy(stage_l.at[j % 2], lo_out.at[:, cols], lo_sem.at[j % 2]),
+            pltpu.make_async_copy(stage_h.at[e % 2], hi_out.at[:, cols], hi_sem.at[e % 2]),
+            pltpu.make_async_copy(stage_l.at[e % 2], lo_out.at[:, cols], lo_sem.at[e % 2]),
         )
 
-    def eliminate_side(j):
+    def eliminate_side(e):
         @pl.when(k != root_k)
         def _():
             @pl.loop(0, nc)
             def _(c):
-                col_arrived(c, j)
+                for b in range(sub):
+                    col_arrived(c, e * sub + b)
 
         @pl.when(is_root)
         def _():
             @pl.loop(0, nc)
             def _(c):
-                pltpu.make_async_copy(col_raw.at[c, j], col_raw.at[c, j], root_sem.at[c, j]).wait()
-
-        @pl.when(j >= 2)
-        def _():
-            for copy in side_copies(j - 2):
+                for b in range(sub):
+                    ref = col_raw.at[c, e * sub + b]
+                    pltpu.make_async_copy(ref, ref, root_sem.at[c, e * sub + b]).wait()
+
+        @pl.when(e >= 2)
+        def _():
+            for copy in side_copies(e - 2):
                 copy.wait()
-        parts = chunk_parts(col_raw, j)
-
-        @pl.loop(0, panels)
-        def _(p):
-            part = pl.ds(pl.multiple_of(p * width, width), width)
-            stage_h[j % 2, part, :], stage_l[j % 2, part, :] = split(scaled_tile(parts, part).T)
-        for copy in side_copies(j):
+        parts = chunk_parts(col_raw, e)
+        for p in range(0, panels, WIDE):
+            stage_h[e % 2, panel(p, WIDE), :], stage_l[e % 2, panel(p, WIDE), :] = split(
+                scaled_tile(parts, panel(p, WIDE)).T)
+        for copy in side_copies(e):
             copy.start()
 
     first = max(reach - 1, 3)
@@ -454,7 +566,7 @@
 
             @pl.when((dist >= 1) & (i >= 0) & (i < nch))
             def _():
-                pltpu.make_async_copy(raw_all.at[c, i], raw_all.at[c, i], raw_recv.at[c, i]).wait()
+                raw_arrived(c, i)
                 raw_step(c, i, raw_all.at[c, i])
 
         @pl.when(at_root_core & (y != root_y))
@@ -462,9 +574,9 @@
             @pl.loop(0, nc)
             def _(c):
                 dist = jnp.abs(c // xs - z) + jnp.abs(c % xs - x)
-                j = s - (jnp.maximum(dist, 1) - 1) - jnp.abs(y - root_y) - half * hch
-
-                @pl.when((j >= 0) & (j < hch))
+                j, mine = side_of(s - (jnp.maximum(dist, 1) - 1) - jnp.abs(y - root_y))
+
+                @pl.when(mine)
                 def _():
                     col_arrived(c, j)
                     src = col_raw.at[c, j]
@@ -484,23 +596,24 @@
         @pl.when(s == len(work) - 1)
         def _():
             spread()
+            masks()
             keep_raw.wait()
 
         i = s - first
 
-        @pl.when((i >= 0) & (i < nch))
-        def _():
-            eliminate(i)
-        j = s - side_lag - half * hch
-
-        @pl.when((j >= 0) & (j < hch))
-        def _():
-            eliminate_side(j)
-
-    for i in range(max(nch - 2, 0), nch):
-        cols_copy(i).wait()
-    for j in range(max(hch - 2, 0), hch):
-        for copy in side_copies(j):
+        @pl.when((i >= 0) & (i < nch) & (i % sub == sub - 1))
+        def _():
+            eliminate(i // sub)
+        j, mine = side_of(s - side_lag)
+
+        @pl.when(mine & (j % sub == sub - 1))
+        def _():
+            eliminate_side(j // sub)
+
+    for e in range(max(nch // sub - 2, 0), nch // sub):
+        cols_copy(e).wait()
+    for e in range(max(hch // sub - 2, 0), hch // sub):
+        for copy in side_copies(e):
             copy.wait()
 
     @pl.loop(0, ys * nc)
@@ -517,25 +630,14 @@
 
     @pl.loop(0, nc)
     def _(c):
-        for (way, late), (_, early) in zip(raw_ways(c, False), raw_ways(c, True)):
-            sem = raw_send.at[way, c]
-
-            @pl.when(late & early)
-            def _(sem=sem):
-                sent(raw_all.at[c], sem)
-
-            if x_first:
-                @pl.when(jnp.logical_not(late) & early)
-                def _(sem=sem):
-                    sent(raw_all.at[c, pl.ds(0, x_first)], sem)
-
-                @pl.when(late & jnp.logical_not(early))
-                def _(sem=sem):
-                    sent(raw_all.at[c, pl.ds(x_first, nch - x_first)], sem)
-            else:
-                @pl.when(late & jnp.logical_not(early))
-                def _(sem=sem):
-                    sent(raw_all.at[c], sem)
+        for way, cond, line, part in raw_ways(c):
+            @pl.when(cond & line)
+            def _(way=way):
+                sent(raw_all.at[c], raw_send.at[way, c])
+
+            @pl.when(cond & jnp.logical_not(line))
+            def _(way=way, part=part):
+                sent(raw_all.at[c, :, part], raw_send.at[way, c])
 
         @pl.when(is_root | (at_root_core & (y > root_y)))
         def _():
@@ -569,27 +671,30 @@
     nch, high, wide = raw.shape
     panels, width, _ = linv.shape
     slots = panels * width
-    rows = nch * CHUNK
+    rows = nch * COMM
     halves = rows // cols
     ys = n_row // 2
     xs = ys if n_col % ys == 0 else 1
     zs = n_col // xs
     hch = nch // halves
-    x_first = nch // 6
-    kall = n_col * (wide + nd)
+    x_rows = (high + 47) // 48 * 8
+    kraw = n_col * wide
+    kall = kraw + n_col * nd
     early = slots - width
     vmem = pl.BlockSpec(memory_space=pltpu.VMEM)
     hbm = pl.BlockSpec(memory_space=pl.ANY)
     dma = pltpu.SemaphoreType.DMA
     return pl.pallas_call(
-        functools.partial(gather_kernel, (zs, xs, ys, halves, per_row, nd, x_first)),
+        functools.partial(gather_kernel, (zs, xs, ys, halves, per_row, nd, x_rows)),
         out_shape=(
             jax.ShapeDtypeStruct((rows, slots), F32),
             jax.ShapeDtypeStruct((slots, cols), BF16),
             jax.ShapeDtypeStruct((slots, cols), BF16),
+            jax.ShapeDtypeStruct((rows, 1), F32),
+            jax.ShapeDtypeStruct((1, cols), F32),
         ),
         in_specs=[vmem] * 6,
-        out_specs=(hbm, hbm, hbm),
+        out_specs=(hbm, hbm, hbm, vmem, vmem),
         scratch_shapes=[
             pltpu.VMEM((n_col, nch, high, wide), F32),
             pltpu.VMEM((n_col, hch, high, wide), F32),
@@ -602,14 +707,14 @@
             pltpu.VMEM((slots, slots), BF16),
             pltpu.VMEM((slots, slots), BF16),
             pltpu.VMEM((early, early), F32),
-            pltpu.VMEM((kall, slots), BF16),
-            pltpu.VMEM((kall, slots), BF16),
+            pltpu.VMEM((kraw + 3 * n_col * nd, slots), BF16),
+            pltpu.VMEM((kraw, slots), BF16),
             pltpu.VMEM((2, CHUNK, slots), F32),
             pltpu.VMEM((2, slots, CHUNK), BF16),
             pltpu.VMEM((2, slots, CHUNK), BF16),
             dma((2,)),
             dma((n_col, hch)),
-            dma((n_col, nch)),
+            dma((n_col, nch, 2)),
             dma((4, n_col)),
             dma((n_col, hch)),
             dma((3, n_col)),
@@ -625,19 +730,14 @@
     )(raw, piv, linv, coef, irow, icol)
 
 
-def trailing_kernel(tile, c_ref, hi_ref, lo_ref, front_ref, rkeep_ref, ckeep_ref, out_ref, factor_ref):
-    cols = hi_ref.shape[1]
+def trailing_kernel(c_ref, hi_ref, lo_ref, front_ref, rkeep_ref, ckeep_ref, out_ref, factor_ref):
     columns = c_ref[...]
     factor_ref[...] = columns
     hi, lo = split(columns)
-    rkeep = rkeep_ref[...] > 0.0
-
-    @pl.loop(0, cols // tile)
-    def _(i):
-        part = pl.ds(pl.multiple_of(i * tile, tile), tile)
-        bh, bl = hi_ref[:, part], lo_ref[:, part]
-        acc = mm(hi, bh) + mm(hi, bl) + mm(lo, bh)
-        out_ref[:, part] = jnp.where(rkeep & (ckeep_ref[:, part] > 0.0), front_ref[:, part] - acc, 0.0)
+    bh = hi_ref[...]
+    acc = mm(hi, bh) + mm(hi, lo_ref[...]) + mm(lo, bh)
+    keep = (rkeep_ref[...] > 0.0) & (ckeep_ref[...] > 0.0)
+    out_ref[...] = jnp.where(keep, front_ref[...] - acc, 0.0)
 
 
 def update(columns, side_hi, side_lo, front, row_keep, col_keep):
@@ -645,7 +745,7 @@
     slots = columns.shape[1]
     tile = 256
     return pl.pallas_call(
-        functools.partial(trailing_kernel, tile),
+        trailing_kernel,
         grid=(rows // tile,),
         in_specs=[
             pl.BlockSpec((tile, slots), lambda i: (i, 0)),
@@ -671,44 +771,16 @@
     n_col = lax.axis_size("col")
     n_row = lax.axis_size("row")
     rows, cols = front.shape
-    row_id = lax.axis_index("row")
-    col_id = lax.axis_index("col")
-    row_start = row_id * rows
-    col_start = col_id * cols
     panels, width, _ = linv.shape
     slots = pivots.shape[0]
     per_col = slots // n_col
     per_row = slots // n_row
     wide = (per_col + LANES - 1) // LANES * LANES
     nd = delayed.shape[0]
-    slot_ids = jnp.arange(slots, dtype=jnp.int32)
-
-    col_owner = pivots // cols
-    row_owner = pivots // rows
-    before = slot_ids[None, :] < slot_ids[:, None]
-    col_rank = jnp.sum((before & (col_owner[:, None] == col_owner[None, :])).astype(jnp.int32), axis=1)
-    row_rank = jnp.sum((before & (row_owner[:, None] == row_owner[None, :])).astype(jnp.int32), axis=1)
-    col_pos = col_owner * wide + col_rank
-    row_pos = row_owner * per_row + row_rank
-    pad = jnp.zeros_like(pivots)
-    irow = jnp.stack([pivots - col_start, row_pos - row_id * per_row, col_pos] + [pad] * 5)
-    icol = jnp.stack([pivots - row_start, col_pos - col_id * wide, row_pos] + [pad] * 5, axis=1)
-
-    in_panel = slot_ids % width
-    coupled = pair_flags.astype(F32) * dinv_off
-    zero = jnp.zeros_like(dinv_diag)
-    coef = jnp.stack(
-        [dinv_diag, jnp.where(in_panel == width - 1, 0.0, coupled), jnp.where(in_panel == 0, 0.0, jnp.roll(coupled, 1))]
-        + [zero] * 5
-    )
-    row_in = jnp.any((row_start + jnp.arange(rows))[:, None] == pivots[None, :], axis=1)
-    col_in = jnp.any((col_start + jnp.arange(cols))[:, None] == pivots[None, :], axis=1)
-    row_keep = jnp.where(row_in, 0.0, 1.0)[:, None]
-    col_keep = jnp.where(col_in, 0.0, 1.0)[None, :]
-
-    dest_wide = jnp.broadcast_to(dest.astype(F32)[:, None], (nd, wide))
-    raw, piv = pick_columns(front, delayed, dest_wide, irow, icol, wide, per_row)
-    columns, side_hi, side_lo = gather(raw, piv, linv, coef, irow, icol, cols, per_row, nd)
+    ids = jnp.stack([pivots, pair_flags])
+    dinv = jnp.stack([dinv_diag, dinv_off])
+    raw, piv, irow, icol, coef = pick_columns(front, delayed, dest[None, :], ids, dinv, n_row, n_col, wide, width)
+    columns, side_hi, side_lo, row_keep, col_keep = gather(raw, piv, linv, coef, irow, icol, cols, per_row, nd)
     trailing, factor = update(columns, side_hi, side_lo, front, row_keep, col_keep)
     return (trailing, factor)
 

time: 293 us -> 238 us (0.81)
  Pallas kernels: 272 us -> 234 us
  other arithmetic: 10.2 us -> 2.62 us
  local copies, waits for them, and re-layouts: 6.56 us -> 0 us
    pallas_call x1, Pallas kernels: 201 us -> 179 us  [gather(): pl.pallas_call(functools.partial(gather_kernel, (zs, xs, ys, halves, per_...]
    pallas_call x2, Pallas kernels: 71 us -> 54.9 us  [the longest x1 37 us: update(): pl.pallas_call(trailing_kernel, grid=(rows // tile,), in_specs=[pl.BlockS...]
    reduce_or x2 -> x0, other arithmetic: 4.35 us -> none  [the longest x1 2.69 us: body(): jnp.any((row_start + jnp.arange(rows))[:, None] == pivots[None, :], axis=1)]
    another operation x9 -> x0, local copies, waits for them, and re-layouts: 3.03 us -> none  [the longest x2 1.32 us: body(): jnp.stack([dinv_diag, jnp.where(in_panel == width - 1, 0.0, coupled), jnp...]
where the time goes in v2:
time: 238 us; the launch traced here: 237 us
  Pallas kernels  234 us (98%)
  other arithmetic  2.62 us (1%)
    pallas_call x1, Pallas kernels, gather(): pl.pallas_call(functools.partial(gather_kernel, (zs, xs, ys, halves, per_...  179 us
    pallas_call x1, Pallas kernels, update(): pl.pallas_call(trailing_kernel, grid=(rows // tile,), in_specs=[pl.BlockS...  37 us
    pallas_call x1, Pallas kernels, pick_columns(): pl.pallas_call(functools.partial(pick_kernel, dims), grid=(n,), in_specs=...  17.8 us

profile of v2, /device:TPU:7, one launch (start us, length us, event | category | flops | bytes accessed | tf_op | source)
XLA Modules:
  0.0 237.1 jit_solution(3557644302303359517)
XLA Ops:
  0.6 1.3 pad_add_fusion.ids_ref
  1.9 1.3 pad_maximum_fusion.dinv_ref
  3.2 17.8 %shard_map.95 = (f32[12,272,128]{2,1,0:T(8,128)}, f32[280,128]{1,0:T(8,128)}, f32[8,1024]{1,0:T(8,128)}, f32[1024,8]{1,0:T(8,128)}, f32[8,1024]{1,0:T(8,128)}) custom-call(f32[3072,1536]{1,0:T(8,128)} %front_ref.3, f32[8,3072]{1,0:T(8,128)} %delayed_ref.1, s32[1,8]{1,0:T(1,128)} %bitcast.9, s32[2,1024]{1,0:T(2,128)} %pad_add_fusion.ids_ref, ...), custom_call_target="tpu_custom_call" | custom-call | tf_op jit(solution)/shard_map/pallas_call | solution.py:153
  21.1 179.0 %shard_map.96 = (f32[3072,1024]{1,0:T(8,128)}, bf16[1024,1536]{1,0:T(8,128)(2,1)}, bf16[1024,1536]{1,0:T(8,128)(2,1)}, f32[3072,1]{1,0:T(8,128)}, f32[1,1536]{1,0:T(1,128)}) custom-call(f32[12,272,128]{2,1,0:T(8,128)} %get-tuple-element.12.raw_own, f32[280,128]{1,0:T(8,128)} %get-tuple-element.13.piv_own, f32[4,256,256]{2,1,0:T(8,128)} %linv_ref.1, ...), custom_call_target="tpu_custom_call" | custom-call | tf_op jit(solution)/shard_map/pallas_call | solution.py:687
  200.1 37.0 %shard_map.97 = (f32[3072,1536]{1,0:T(8,128)}, f32[3072,1024]{1,0:T(8,128)}) custom-call(f32[3072,1024]{1,0:T(8,128)} %get-tuple-element.17.c_ref, bf16[1024,1536]{1,0:T(8,128)(2,1)} %get-tuple-element.18.hi_ref, bf16[1024,1536]{1,0:T(8,128)(2,1)} %get-tuple-element.19.lo_ref, f32[3072,1536]{1,0:T(8,128)} %front_ref.3, ...), custom_call_target="tpu_custom_call" | custom-call | tf_op jit(solution)/shard_map/pallas_call | solution.py:747

commit v3 on v2

--- a/solution.py
+++ b/solution.py
@@ -8,11 +8,12 @@
 from jax.sharding import PartitionSpec as P
 
 MESH = pl.DeviceIdType.MESH
-VMEM_LIMIT = 62 * 1024 * 1024
+VMEM_LIMIT = 66_800_000
 F32 = jnp.float32
 BF16 = jnp.bfloat16
 CHUNK = 256
 COMM = 256
+EARLY = 4
 WIDE = 4
 LANES = 128
 
@@ -60,144 +61,58 @@
     return jnp.broadcast_to(row, (8, row.shape[1])).T[:, 0:1]
 
 
-def pick_kernel(
-    dims, front_ref, delayed_ref, dest_ref, ids_ref, dinv_ref,
-    raw_ref, piv_ref, irow_ref, icol_ref, coef_ref, g_ref, want_ref, acc_ref, dacc_ref,
-):
-    n_row, n_col, rows, width, per_col = dims
-    i = pl.program_id(0)
+def index_tables(dims, row_id, col_id, ids_ref, dinv_ref, irow_ref, icol_ref, coef_ref, g_ref, want_ref):
+    n_row, n_col, rows, cols, width, per_col = dims
     slots = ids_ref.shape[1]
-    cols, wide = g_ref.shape
+    wide = g_ref.shape[1]
     per_row = want_ref.shape[0]
-    nd = delayed_ref.shape[0]
-    tile = front_ref.shape[0]
-    high = raw_ref.shape[1]
-    ch = tile // raw_ref.shape[0]
-    row_id, col_id = lax.axis_index("row"), lax.axis_index("col")
-
-    @pl.when(i == 0)
-    def _():
-        piv = ids_ref[0:1, :].astype(F32)
-        col_owner = owner_of(piv, cols, n_col)
-        row_owner = owner_of(piv, rows, n_row)
-        col_pos = col_owner * wide + rank_of(col_owner, turned(col_owner))
-        row_pos = row_owner * per_row + rank_of(row_owner, turned(row_owner))
-        piv_col = turned(piv)
-        row_pos_col, col_pos_col = turned(row_pos), turned(col_pos)
-        irow_ref[...] = jnp.zeros_like(irow_ref)
-        irow_ref[0:1, :] = piv
-        irow_ref[1:2, :] = col_pos
-        icol_ref[...] = jnp.zeros_like(icol_ref)
-        icol_ref[:, 0:1] = row_pos_col
-        icol_ref[:, 1:2] = piv_col
-
-        mine = col_pos_col - (col_id * wide).astype(F32) == iota((slots, wide), 1).astype(F32)
-        want_col = jnp.sum(jnp.where(mine, piv_col - (col_id * cols).astype(F32), 0.0), axis=0, keepdims=True)
-        real = iota((1, wide), 1) < per_col
-        want_col = jnp.where(real, want_col, -1.0)
-        g_ref[...] = one_hot(iota((cols, wide), 0).astype(F32) == want_col)
-        mine = row_pos - (row_id * per_row).astype(F32) == iota((per_row, slots), 0).astype(F32)
-        want_ref[...] = jnp.sum(jnp.where(mine, piv - (row_id * rows).astype(F32), 0.0), axis=1, keepdims=True)
-
-        slot = iota((1, slots), 1) % width
-        coupled = ids_ref[1:2, :].astype(F32) * dinv_ref[1:2, :]
-        coef_ref[...] = jnp.zeros_like(coef_ref)
-        coef_ref[0:1, :] = dinv_ref[0:1, :]
-        coef_ref[1:2, :] = jnp.where(slot == width - 1, 0.0, coupled)
-        coef_ref[2:3, :] = jnp.where(slot == 0, 0.0, pltpu.roll(jnp.broadcast_to(coupled, (8, slots)), 1, 1)[0:1, :])
-        acc_ref[...] = jnp.zeros_like(acc_ref)
-        dacc_ref[...] = jnp.zeros_like(dacc_ref)
-
-    hi, lo = split(front_ref[...])
-    g = g_ref[...]
-    raw = mm(hi, g) + mm(lo, g)
-    for b in range(raw_ref.shape[0]):
-        raw_ref[b, :ch, :] = raw[b * ch : (b + 1) * ch, :]
-        for t in range(ch // LANES):
-            at = b * ch + t * LANES
-            raw_ref[b, ch + t * nd : ch + (t + 1) * nd, :] = delayed_ref[:, at : at + LANES]
-
-    start = row_tile(i, rows // tile, rows // cols) * tile
-    sel = one_hot(want_ref[...].astype(jnp.int32) - start == iota((per_row, tile), 1))
-    rh, rl = split(raw)
-    acc_ref[...] += mm(sel, rh) + mm(sel, rl)
-    dh, dl = split(delayed_ref[...])
-    dacc_ref[...] += mm_t(dh, sel) + mm_t(dl, sel)
-
-    @pl.when(i == pl.num_programs(0) - 1)
-    def _():
-        piv_ref[:per_row, :] = acc_ref[...]
-        for b in range(per_row // LANES):
-            piv_ref[per_row + b * nd : per_row + (b + 1) * nd, :] = dacc_ref[:, b * LANES : (b + 1) * LANES]
-        diagonal = iota((nd, nd), 0) == iota((nd, nd), 1)
-        dest = jnp.sum(jnp.where(diagonal, dest_ref[...].astype(F32), 0.0), axis=1, keepdims=True)
-        piv_ref[per_row + per_row // LANES * nd :, :] = jnp.broadcast_to(dest, (nd, wide))
+    piv = ids_ref[0:1, :].astype(F32)
+    col_owner = owner_of(piv, cols, n_col)
+    row_owner = owner_of(piv, rows, n_row)
+    col_pos = col_owner * wide + rank_of(col_owner, turned(col_owner))
+    row_pos = row_owner * per_row + rank_of(row_owner, turned(row_owner))
+    piv_col = turned(piv)
+    col_pos_col = turned(col_pos)
+    irow_ref[...] = jnp.zeros_like(irow_ref)
+    irow_ref[0:1, :] = piv
+    irow_ref[1:2, :] = col_pos
+    icol_ref[...] = jnp.zeros_like(icol_ref)
+    icol_ref[:, 0:1] = turned(row_pos)
+    icol_ref[:, 1:2] = piv_col
+
+    mine = col_pos_col - (col_id * wide).astype(F32) == iota((slots, wide), 1).astype(F32)
+    want_col = jnp.sum(jnp.where(mine, piv_col - (col_id * cols).astype(F32), 0.0), axis=0, keepdims=True)
+    want_col = jnp.where(iota((1, wide), 1) < per_col, want_col, -1.0)
+    g_ref[...] = one_hot(iota((cols, wide), 0).astype(F32) == want_col)
+    mine = row_pos - (row_id * per_row).astype(F32) == iota((per_row, slots), 0).astype(F32)
+    want_ref[...] = jnp.sum(jnp.where(mine, piv - (row_id * rows).astype(F32), 0.0), axis=1, keepdims=True)
+
+    slot = iota((1, slots), 1) % width
+    coupled = ids_ref[1:2, :].astype(F32) * dinv_ref[1:2, :]
+    coef_ref[...] = jnp.zeros_like(coef_ref)
+    coef_ref[0:1, :] = dinv_ref[0:1, :]
+    coef_ref[1:2, :] = jnp.where(slot == width - 1, 0.0, coupled)
+    coef_ref[2:3, :] = jnp.where(slot == 0, 0.0, pltpu.roll(jnp.broadcast_to(coupled, (8, slots)), 1, 1)[0:1, :])
 
 
 def row_tile(i, tiles, halves):
     return i % halves * (tiles // halves) + i // halves
 
 
-def pick_columns(front, delayed, dest, ids, dinv, n_row, n_col, wide, width):
-    rows, cols = front.shape
-    nd = delayed.shape[0]
-    slots = ids.shape[1]
-    per_row = slots // n_row
-    halves = rows // cols
-    tile = CHUNK
-    n = rows // tile
-    sub = tile // COMM
-    high = COMM + nd * (COMM // LANES)
-    piv_high = per_row + nd * (per_row // LANES) + nd
-    dims = (n_row, n_col, rows, width, slots // n_col)
-    return pl.pallas_call(
-        functools.partial(pick_kernel, dims),
-        grid=(n,),
-        in_specs=[
-            pl.BlockSpec((tile, cols), lambda i: (row_tile(i, n, halves), 0)),
-            pl.BlockSpec((nd, tile), lambda i: (0, row_tile(i, n, halves))),
-            pl.BlockSpec((1, nd), lambda i: (0, 0)),
-            pl.BlockSpec((2, slots), lambda i: (0, 0)),
-            pl.BlockSpec((2, slots), lambda i: (0, 0)),
-        ],
-        out_specs=(
-            pl.BlockSpec((sub, high, wide), lambda i: (i, 0, 0)),
-            pl.BlockSpec((piv_high, wide), lambda i: (0, 0)),
-            pl.BlockSpec((8, slots), lambda i: (0, 0)),
-            pl.BlockSpec((slots, 8), lambda i: (0, 0)),
-            pl.BlockSpec((8, slots), lambda i: (0, 0)),
-        ),
-        out_shape=(
-            jax.ShapeDtypeStruct((n * sub, high, wide), F32),
-            jax.ShapeDtypeStruct((piv_high, wide), F32),
-            jax.ShapeDtypeStruct((8, slots), F32),
-            jax.ShapeDtypeStruct((slots, 8), F32),
-            jax.ShapeDtypeStruct((8, slots), F32),
-        ),
-        scratch_shapes=[
-            pltpu.VMEM((cols, wide), BF16),
-            pltpu.VMEM((per_row, 1), F32),
-            pltpu.VMEM((per_row, wide), F32),
-            pltpu.VMEM((nd, per_row), F32),
-        ],
-        compiler_params=pltpu.CompilerParams(dimension_semantics=("arbitrary",), vmem_limit_bytes=VMEM_LIMIT),
-    )(front, delayed, dest, ids, dinv)
-
-
 def gather_kernel(
-    dims, raw_own, piv_own, linv_ref, coef_ref, irow_ref, icol_ref,
+    dims, front_ref, delayed_ref, dest_ref, ids_ref, dinv_ref, linv_ref,
     cols_out, hi_out, lo_out, rkeep_ref, ckeep_ref,
+    irow_ref, icol_ref, coef_ref, g_ref, want_ref, acc_ref, dacc_ref, fbuf,
     raw_all, col_raw, piv_all, rowperm, t1h, t1l, qh, ql, nh, nl, rd, mh, ml, stage, stage_h, stage_l,
-    keep_sem, root_sem, raw_recv, raw_send, col_recv, col_send, piv_recv, piv_send, out_sem, hi_sem, lo_sem,
+    front_sem, root_sem, raw_recv, raw_send, col_recv, col_send, piv_recv, piv_send, out_sem, hi_sem, lo_sem,
 ):
     zs, xs, ys, halves, per_row, nd, x_rows = dims
     nc, n_row = zs * xs, ys * 2
-    nch = raw_own.shape[0]
-    high = raw_own.shape[1]
+    nch, high, wide = raw_all.shape[1:]
+    rows, cols = front_ref.shape
     hch = nch // halves
     panels, width, _ = linv_ref.shape
     slots = panels * width
-    wide = raw_own.shape[2]
     ch = COMM
     sub = CHUNK // COMM
     z_part, x_part = pl.ds(0, high - x_rows), pl.ds(high - x_rows, x_rows)
@@ -226,6 +141,10 @@
         (None, at(y, 1 - k, z, x)),
     ]
 
+    for i in range(min(2, nch)):
+        tile = pl.ds(row_tile(i, nch, halves) * CHUNK, CHUNK)
+        pltpu.make_async_copy(front_ref.at[tile, :], fbuf.at[i], front_sem.at[i]).start()
+
     barrier = pltpu.get_barrier_semaphore()
     peers = 1
     for cond, dev in links:
@@ -329,19 +248,63 @@
     def col_arrived(c, j):
         pltpu.make_async_copy(col_raw.at[c, j], col_raw.at[c, j], col_recv.at[c, j]).wait()
 
-    keep_raw = pltpu.make_async_copy(raw_own, raw_all.at[col], keep_sem.at[0])
-    keep_piv = pltpu.make_async_copy(piv_own, piv_all.at[row, col], keep_sem.at[1])
-    keep_raw.start()
-    keep_piv.start()
+    own_piv = piv_all.at[row, col]
 
     def own_step(i):
         @pl.when(i < nch)
         def _():
-            raw_step(col, i, raw_own.at[i])
-
-    piv_step(y, col, piv_own)
-    own_step(0)
-    ahead = 1
+            raw_step(col, i, raw_all.at[col, i])
+
+    def front_copy(i):
+        tile = pl.ds(pl.multiple_of(row_tile(i, nch, halves) * CHUNK, CHUNK), CHUNK)
+        return pltpu.make_async_copy(front_ref.at[tile, :], fbuf.at[i % 3], front_sem.at[i % 3])
+
+    def pick(i):
+        hi, lo = split(fbuf[i % 3])
+        g = g_ref[...]
+        raw_all[col, i, :ch, :] = mm(hi, g) + mm(lo, g)
+        start = row_tile(i, nch, halves) * CHUNK
+        for t in range(ch // LANES):
+            part = pl.ds(pl.multiple_of(start + t * LANES, LANES), LANES)
+            raw_all[col, i, ch + t * nd : ch + (t + 1) * nd, :] = delayed_ref[:, part]
+
+    def pick_rows(i):
+        start = row_tile(i, nch, halves) * CHUNK
+        sel = one_hot(want_ref[...].astype(jnp.int32) - start == iota((per_row, ch), 1))
+        rh, rl = split(raw_all[col, i, :ch, :])
+        acc_ref[...] += mm(sel, rh) + mm(sel, rl)
+        dh, dl = split(delayed_ref[:, pl.ds(pl.multiple_of(start, CHUNK), ch)])
+        dacc_ref[...] += mm_t(dh, sel) + mm_t(dl, sel)
+
+    index_tables(
+        (n_row, nc, rows, cols, width, slots // nc), row, col, ids_ref, dinv_ref, irow_ref, icol_ref, coef_ref, g_ref, want_ref)
+    acc_ref[...] = jnp.zeros_like(acc_ref)
+    dacc_ref[...] = jnp.zeros_like(dacc_ref)
+
+    @pl.loop(0, nch)
+    def _(i):
+        @pl.when(i + 2 < nch)
+        def _():
+            front_copy(i + 2).start()
+        front_copy(i).wait()
+        pick(i)
+
+        @pl.when(i > 0)
+        def _():
+            @pl.when(i <= EARLY)
+            def _():
+                own_step(i - 1)
+            pick_rows(i - 1)
+    pick_rows(nch - 1)
+    piv_all[row, col, :per_row, :] = acc_ref[...]
+    for b in range(per_row // LANES):
+        piv_all[row, col, per_row + b * nd : per_row + (b + 1) * nd, :] = dacc_ref[:, b * LANES : (b + 1) * LANES]
+    diagonal = iota((nd, nd), 0) == iota((nd, nd), 1)
+    dest = jnp.sum(jnp.where(diagonal, dest_ref[...].astype(F32), 0.0), axis=1, keepdims=True)
+    piv_all[row, col, per_row + per_row // LANES * nd :, :] = jnp.broadcast_to(dest, (nd, wide))
+
+    own_step(EARLY)
+    piv_step(y, col, own_piv)
 
     @pl.loop(1, span + 1)
     def _(s):
@@ -354,33 +317,28 @@
             def _():
                 piv_arrived(sy * 2 + k, c)
                 piv_step(sy, c, piv_all.at[sy * 2 + k, c])
-        own_step(s)
-    ahead = span + 1
+        own_step(EARLY + s)
+    ahead = EARLY + span + 1
 
     def panel(p, n=1):
         return slice(p * width, (p + n) * width)
 
-    def masks():
-        n = ckeep_ref.shape[1] // CHUNK
-
-        @pl.loop(0, n)
-        def _(t):
-            ids = iota((slots, CHUNK), 1) + t * CHUNK + col * (n * CHUNK)
+    def masks(t):
+        at_tile = pl.ds(pl.multiple_of(t * CHUNK, CHUNK), CHUNK)
+
+        @pl.when(t < cols // CHUNK)
+        def _():
+            ids = iota((slots, CHUNK), 1) + t * CHUNK + col * cols
             hit = jnp.where(icol_ref[:, 1:2].astype(jnp.int32) == ids, 1.0, 0.0)
-            ckeep_ref[:, pl.ds(pl.multiple_of(t * CHUNK, CHUNK), CHUNK)] = 1.0 - jnp.max(hit, axis=0, keepdims=True)
-        n = rkeep_ref.shape[0] // CHUNK
-
-        @pl.loop(0, n)
-        def _(t):
-            ids = iota((CHUNK, slots), 0) + t * CHUNK + row * (n * CHUNK)
-            hit = jnp.where(irow_ref[0:1, :].astype(jnp.int32) == ids, 1.0, 0.0)
-            rkeep_ref[pl.ds(pl.multiple_of(t * CHUNK, CHUNK), CHUNK), :] = 1.0 - jnp.max(hit, axis=1, keepdims=True)
+            ckeep_ref[:, at_tile] = 1.0 - jnp.max(hit, axis=0, keepdims=True)
+        ids = iota((CHUNK, slots), 0) + t * CHUNK + row * rows
+        hit = jnp.where(irow_ref[0:1, :].astype(jnp.int32) == ids, 1.0, 0.0)
+        rkeep_ref[at_tile, :] = 1.0 - jnp.max(hit, axis=1, keepdims=True)
 
     def gather_square():
         @pl.loop(0, ys * nc)
         def _(q):
             piv_arrived((q // nc) * 2 + 1 - k, q % nc)
-        keep_piv.wait()
 
         @pl.loop(0, panels - 1)
         def _(p):
@@ -553,7 +511,7 @@
 
     first = max(reach - 1, 3)
     side_lag = reach - 1 + ys
-    work = [gather_square, square, recur]
+    work = [gather_square, square, recur, spread]
 
     @pl.loop(0, nch + max(first, side_lag))
     def _(s):
@@ -593,11 +551,9 @@
         for n, piece in enumerate(work):
             pl.when(s == n)(piece)
 
-        @pl.when(s == len(work) - 1)
-        def _():
-            spread()
-            masks()
-            keep_raw.wait()
+        @pl.when(s < rows // CHUNK)
+        def _():
+            masks(s)
 
         i = s - first
 
@@ -622,8 +578,8 @@
         for way, cond in piv_ways(sy, c):
             @pl.when(cond)
             def _(way=way):
-                piv_copy(way, sy, c, piv_own).wait_send()
-        piv_copy(6, sy, c, piv_own).wait_send()
+                piv_copy(way, sy, c, own_piv).wait_send()
+        piv_copy(6, sy, c, own_piv).wait_send()
 
     def sent(ref, sem):
         pltpu.make_async_copy(ref, ref, sem).wait()
@@ -665,13 +621,19 @@
     )
 
 
-def gather(raw, piv, linv, coef, irow, icol, cols, per_row, nd):
+def gather(front, delayed, dest, ids, dinv, linv):
     n_col = lax.axis_size("col")
     n_row = lax.axis_size("row")
-    nch, high, wide = raw.shape
+    rows, cols = front.shape
+    nd = delayed.shape[0]
     panels, width, _ = linv.shape
     slots = panels * width
-    rows = nch * COMM
+    per_col = slots // n_col
+    per_row = slots // n_row
+    wide = (per_col + LANES - 1) // LANES * LANES
+    nch = rows // COMM
+    high = COMM + nd * (COMM // LANES)
+    piv_high = per_row + nd * (per_row // LANES) + nd
     halves = rows // cols
     ys = n_row // 2
     xs = ys if n_col % ys == 0 else 1
@@ -693,12 +655,20 @@
             jax.ShapeDtypeStruct((rows, 1), F32),
             jax.ShapeDtypeStruct((1, cols), F32),
         ),
-        in_specs=[vmem] * 6,
+        in_specs=[hbm] + [vmem] * 5,
         out_specs=(hbm, hbm, hbm, vmem, vmem),
         scratch_shapes=[
+            pltpu.VMEM((8, slots), F32),
+            pltpu.VMEM((slots, 8), F32),
+            pltpu.VMEM((8, slots), F32),
+            pltpu.VMEM((cols, wide), BF16),
+            pltpu.VMEM((per_row, 1), F32),
+            pltpu.VMEM((per_row, wide), F32),
+            pltpu.VMEM((nd, per_row), F32),
+            pltpu.VMEM((3, CHUNK, cols), F32),
             pltpu.VMEM((n_col, nch, high, wide), F32),
             pltpu.VMEM((n_col, hch, high, wide), F32),
-            pltpu.VMEM((n_row, n_col) + piv.shape, F32),
+            pltpu.VMEM((n_row, n_col, piv_high, wide), F32),
             pltpu.VMEM((early, slots), BF16),
             pltpu.VMEM((early, kall), BF16),
             pltpu.VMEM((early, kall), BF16),
@@ -712,7 +682,7 @@
             pltpu.VMEM((2, CHUNK, slots), F32),
             pltpu.VMEM((2, slots, CHUNK), BF16),
             pltpu.VMEM((2, slots, CHUNK), BF16),
-            dma((2,)),
+            dma((3,)),
             dma((n_col, hch)),
             dma((n_col, nch, 2)),
             dma((4, n_col)),
@@ -727,7 +697,7 @@
         compiler_params=pltpu.CompilerParams(
             collective_id=0, has_side_effects=True, vmem_limit_bytes=VMEM_LIMIT
         ),
-    )(raw, piv, linv, coef, irow, icol)
+    )(front, delayed, dest, ids, dinv, linv)
 
 
 def trailing_kernel(c_ref, hi_ref, lo_ref, front_ref, rkeep_ref, ckeep_ref, out_ref, factor_ref):
@@ -768,19 +738,9 @@
 
 
 def body(front, delayed, dest, pivots, pair_flags, linv, dinv_diag, dinv_off):
-    n_col = lax.axis_size("col")
-    n_row = lax.axis_size("row")
-    rows, cols = front.shape
-    panels, width, _ = linv.shape
-    slots = pivots.shape[0]
-    per_col = slots // n_col
-    per_row = slots // n_row
-    wide = (per_col + LANES - 1) // LANES * LANES
-    nd = delayed.shape[0]
     ids = jnp.stack([pivots, pair_flags])
     dinv = jnp.stack([dinv_diag, dinv_off])
-    raw, piv, irow, icol, coef = pick_columns(front, delayed, dest[None, :], ids, dinv, n_row, n_col, wide, width)
-    columns, side_hi, side_lo, row_keep, col_keep = gather(raw, piv, linv, coef, irow, icol, cols, per_row, nd)
+    columns, side_hi, side_lo, row_keep, col_keep = gather(front, delayed, dest[None, :], ids, dinv, linv)
     trailing, factor = update(columns, side_hi, side_lo, front, row_keep, col_keep)
     return (trailing, factor)
 

time: 238 us -> 222 us (0.933)
  Pallas kernels: 234 us -> 218 us
    pallas_call x1 -> x0, Pallas kernels: 17.8 us -> none  [pick_columns(): pl.pallas_call(functools.partial(pick_kernel, dims), grid=(n,), in_specs=...]
where the time goes in v3:
time: 222 us; the launch traced here: 221 us
  Pallas kernels  218 us (98%)
  other arithmetic  2.62 us (1%)
    pallas_call x1, Pallas kernels, gather(): pl.pallas_call(functools.partial(gather_kernel, (zs, xs, ys, halves, per_...  181 us
    pallas_call x1, Pallas kernels, update(): pl.pallas_call(trailing_kernel, grid=(rows // tile,), in_specs=[pl.BlockS...  37 us

profile of v3, /device:TPU:7, one launch (start us, length us, event | category | flops | bytes accessed | tf_op | source)
XLA Modules:
  0.0 221.1 jit_solution(3207951045153288403)
XLA Ops:
  0.6 1.3 pad_add_fusion.ids_ref
  1.9 1.3 pad_maximum_fusion.dinv_ref
  3.3 180.8 %shard_map.95 = (f32[3072,1024]{1,0:T(8,128)}, bf16[1024,1536]{1,0:T(8,128)(2,1)}, bf16[1024,1536]{1,0:T(8,128)(2,1)}, f32[3072,1]{1,0:T(8,128)}, f32[1,1536]{1,0:T(1,128)}) custom-call(f32[3072,1536]{1,0:T(8,128)} %front_ref.3, f32[8,3072]{1,0:T(8,128)} %delayed_ref.1, s32[1,8]{1,0:T(1,128)} %bitcast.9, s32[2,1024]{1,0:T(2,128)} %pad_add_fusion.ids_ref, ...), custom_call_target="tpu_custom_call" | custom-call | tf_op jit(solution)/shard_map/pallas_call | solution.py:649
  184.1 37.0 %shard_map.96 = (f32[3072,1536]{1,0:T(8,128)}, f32[3072,1024]{1,0:T(8,128)}) custom-call(f32[3072,1024]{1,0:T(8,128)} %get-tuple-element.7.c_ref, bf16[1024,1536]{1,0:T(8,128)(2,1)} %get-tuple-element.8.hi_ref, bf16[1024,1536]{1,0:T(8,128)(2,1)} %get-tuple-element.9.lo_ref, f32[3072,1536]{1,0:T(8,128)} %front_ref.3, f32[3072,1]{1,0:T(8,128)} %get-tuple-element.10.rkeep_ref, ...), custom_call_target="tpu_custom_call" | custom-call | tf_op jit(solution)/shard_map/pallas_call | solution.py:717

commit v4 on v3

--- a/solution.py
+++ b/solution.py
@@ -61,36 +61,42 @@
     return jnp.broadcast_to(row, (8, row.shape[1])).T[:, 0:1]
 
 
-def index_tables(dims, row_id, col_id, ids_ref, dinv_ref, irow_ref, icol_ref, coef_ref, g_ref, want_ref):
-    n_row, n_col, rows, cols, width, per_col = dims
-    slots = ids_ref.shape[1]
+def col_tables(dims, col_id, slot_refs, irow_ref, icol_ref, g_ref):
+    _, n_col, _, cols, _, per_col = dims
+    piv_ref = slot_refs[0]
+    slots = piv_ref.shape[1]
     wide = g_ref.shape[1]
-    per_row = want_ref.shape[0]
-    piv = ids_ref[0:1, :].astype(F32)
+    piv = piv_ref[...].astype(F32)
     col_owner = owner_of(piv, cols, n_col)
-    row_owner = owner_of(piv, rows, n_row)
     col_pos = col_owner * wide + rank_of(col_owner, turned(col_owner))
-    row_pos = row_owner * per_row + rank_of(row_owner, turned(row_owner))
     piv_col = turned(piv)
-    col_pos_col = turned(col_pos)
     irow_ref[...] = jnp.zeros_like(irow_ref)
     irow_ref[0:1, :] = piv
     irow_ref[1:2, :] = col_pos
     icol_ref[...] = jnp.zeros_like(icol_ref)
-    icol_ref[:, 0:1] = turned(row_pos)
     icol_ref[:, 1:2] = piv_col
-
-    mine = col_pos_col - (col_id * wide).astype(F32) == iota((slots, wide), 1).astype(F32)
+    mine = turned(col_pos) - (col_id * wide).astype(F32) == iota((slots, wide), 1).astype(F32)
     want_col = jnp.sum(jnp.where(mine, piv_col - (col_id * cols).astype(F32), 0.0), axis=0, keepdims=True)
     want_col = jnp.where(iota((1, wide), 1) < per_col, want_col, -1.0)
     g_ref[...] = one_hot(iota((cols, wide), 0).astype(F32) == want_col)
+
+
+def row_tables(dims, row_id, slot_refs, icol_ref, coef_ref, want_ref):
+    n_row, _, rows, _, width, _ = dims
+    piv_ref, flag_ref, diag_ref, off_ref = slot_refs
+    slots = piv_ref.shape[1]
+    per_row = want_ref.shape[0]
+    piv = piv_ref[...].astype(F32)
+    row_owner = owner_of(piv, rows, n_row)
+    row_pos = row_owner * per_row + rank_of(row_owner, turned(row_owner))
+    icol_ref[:, 0:1] = turned(row_pos)
     mine = row_pos - (row_id * per_row).astype(F32) == iota((per_row, slots), 0).astype(F32)
     want_ref[...] = jnp.sum(jnp.where(mine, piv - (row_id * rows).astype(F32), 0.0), axis=1, keepdims=True)
 
     slot = iota((1, slots), 1) % width
-    coupled = ids_ref[1:2, :].astype(F32) * dinv_ref[1:2, :]
+    coupled = flag_ref[...].astype(F32) * off_ref[...]
     coef_ref[...] = jnp.zeros_like(coef_ref)
-    coef_ref[0:1, :] = dinv_ref[0:1, :]
+    coef_ref[0:1, :] = diag_ref[...]
     coef_ref[1:2, :] = jnp.where(slot == width - 1, 0.0, coupled)
     coef_ref[2:3, :] = jnp.where(slot == 0, 0.0, pltpu.roll(jnp.broadcast_to(coupled, (8, slots)), 1, 1)[0:1, :])
 
@@ -100,10 +106,10 @@
 
 
 def gather_kernel(
-    dims, front_ref, delayed_ref, dest_ref, ids_ref, dinv_ref, linv_ref,
+    dims, front_ref, delayed_ref, dest_ref, piv_ref, flag_ref, diag_ref, off_ref, linv_ref,
     cols_out, hi_out, lo_out, rkeep_ref, ckeep_ref,
     irow_ref, icol_ref, coef_ref, g_ref, want_ref, acc_ref, dacc_ref, fbuf,
-    raw_all, col_raw, piv_all, rowperm, t1h, t1l, qh, ql, nh, nl, rd, mh, ml, stage, stage_h, stage_l,
+    raw_all, col_raw, piv_all, t1h, t1l, qh, ql, nh, nl, rd, mh, ml, stage, stage_h, stage_l,
     front_sem, root_sem, raw_recv, raw_send, col_recv, col_send, piv_recv, piv_send, out_sem, hi_sem, lo_sem,
 ):
     zs, xs, ys, halves, per_row, nd, x_rows = dims
@@ -156,7 +162,6 @@
             @pl.when(cond)
             def _(dev=dev):
                 pl.semaphore_signal(barrier, inc=1, device_id=dev, device_id_type=MESH)
-    pl.semaphore_wait(barrier, peers)
 
     def remote(way, src, dst, send, recv):
         return pltpu.make_async_remote_copy(
@@ -276,8 +281,10 @@
         dh, dl = split(delayed_ref[:, pl.ds(pl.multiple_of(start, CHUNK), ch)])
         dacc_ref[...] += mm_t(dh, sel) + mm_t(dl, sel)
 
-    index_tables(
-        (n_row, nc, rows, cols, width, slots // nc), row, col, ids_ref, dinv_ref, irow_ref, icol_ref, coef_ref, g_ref, want_ref)
+    tables = (n_row, nc, rows, cols, width, slots // nc)
+    slot_refs = (piv_ref, flag_ref, diag_ref, off_ref)
+    col_tables(tables, col, slot_refs, irow_ref, icol_ref, g_ref)
+    pl.semaphore_wait(barrier, peers)
     acc_ref[...] = jnp.zeros_like(acc_ref)
     dacc_ref[...] = jnp.zeros_like(dacc_ref)
 
@@ -294,6 +301,10 @@
             @pl.when(i <= EARLY)
             def _():
                 own_step(i - 1)
+
+            @pl.when(i == 1)
+            def _():
+                row_tables(tables, row, slot_refs, icol_ref, coef_ref, want_ref)
             pick_rows(i - 1)
     pick_rows(nch - 1)
     piv_all[row, col, :per_row, :] = acc_ref[...]
@@ -344,7 +355,7 @@
         def _(p):
             part = pl.ds(pl.multiple_of(p * width, width), width)
             later = pl.ds(pl.multiple_of((p + 1) * width, width), width)
-            rowperm[part, :] = one_hot(icol_ref[later, 0:1].astype(jnp.int32) == iota((width, n_row * per_row), 1))
+            mh[part, :] = one_hot(icol_ref[later, 0:1].astype(jnp.int32) == iota((width, n_row * per_row), 1))
 
         @pl.loop(0, nc // 2)
         def _(c2):
@@ -361,7 +372,7 @@
             @pl.loop(0, panels - 1)
             def _(p):
                 part = pl.ds(pl.multiple_of(p * width, width), width)
-                perm = rowperm[part, :]
+                perm = mh[part, :]
                 a, b = split(mm(perm, h) + mm(perm, l))
                 t1h[part, at_cols] = a
                 t1l[part, at_cols] = b
@@ -381,7 +392,7 @@
         @pl.loop(0, panels - 1)
         def _(p):
             part = pl.ds(pl.multiple_of(p * width, width), width)
-            perm = rowperm[part, :]
+            perm = mh[part, :]
             a, b = split(mm_t(perm, h) + mm_t(perm, l))
             t1h[part, kraw:] = a
             t1l[part, kraw:] = b
@@ -509,8 +520,18 @@
         for copy in side_copies(e):
             copy.start()
 
+    def piv_drain():
+        @pl.loop(0, ys * nc)
+        def _(q):
+            sy, c = q // nc, q % nc
+            for way, cond in piv_ways(sy, c):
+                @pl.when(cond)
+                def _(way=way):
+                    piv_copy(way, sy, c, own_piv).wait_send()
+            piv_copy(6, sy, c, own_piv).wait_send()
+
     first = max(reach - 1, 3)
-    side_lag = reach - 1 + ys
+    side_lag = reach - 2 + ys
     work = [gather_square, square, recur, spread]
 
     @pl.loop(0, nch + max(first, side_lag))
@@ -554,6 +575,8 @@
         @pl.when(s < rows // CHUNK)
         def _():
             masks(s)
+
+        pl.when(s == len(work))(piv_drain)
 
         i = s - first
 
@@ -571,15 +594,6 @@
     for e in range(max(hch // sub - 2, 0), hch // sub):
         for copy in side_copies(e):
             copy.wait()
-
-    @pl.loop(0, ys * nc)
-    def _(q):
-        sy, c = q // nc, q % nc
-        for way, cond in piv_ways(sy, c):
-            @pl.when(cond)
-            def _(way=way):
-                piv_copy(way, sy, c, own_piv).wait_send()
-        piv_copy(6, sy, c, own_piv).wait_send()
 
     def sent(ref, sem):
         pltpu.make_async_copy(ref, ref, sem).wait()
@@ -621,7 +635,7 @@
     )
 
 
-def gather(front, delayed, dest, ids, dinv, linv):
+def gather(front, delayed, dest, pivots, flags, diag, off, linv):
     n_col = lax.axis_size("col")
     n_row = lax.axis_size("row")
     rows, cols = front.shape
@@ -655,7 +669,7 @@
             jax.ShapeDtypeStruct((rows, 1), F32),
             jax.ShapeDtypeStruct((1, cols), F32),
         ),
-        in_specs=[hbm] + [vmem] * 5,
+        in_specs=[hbm] + [vmem] * 7,
         out_specs=(hbm, hbm, hbm, vmem, vmem),
         scratch_shapes=[
             pltpu.VMEM((8, slots), F32),
@@ -669,7 +683,6 @@
             pltpu.VMEM((n_col, nch, high, wide), F32),
             pltpu.VMEM((n_col, hch, high, wide), F32),
             pltpu.VMEM((n_row, n_col, piv_high, wide), F32),
-            pltpu.VMEM((early, slots), BF16),
             pltpu.VMEM((early, kall), BF16),
             pltpu.VMEM((early, kall), BF16),
             pltpu.VMEM((early, early), BF16),
@@ -697,7 +710,7 @@
         compiler_params=pltpu.CompilerParams(
             collective_id=0, has_side_effects=True, vmem_limit_bytes=VMEM_LIMIT
         ),
-    )(front, delayed, dest, ids, dinv, linv)
+    )(front, delayed, dest, pivots, flags, diag, off, linv)
 
 
 def trailing_kernel(c_ref, hi_ref, lo_ref, front_ref, rkeep_ref, ckeep_ref, out_ref, factor_ref):
@@ -738,9 +751,8 @@
 
 
 def body(front, delayed, dest, pivots, pair_flags, linv, dinv_diag, dinv_off):
-    ids = jnp.stack([pivots, pair_flags])
-    dinv = jnp.stack([dinv_diag, dinv_off])
-    columns, side_hi, side_lo, row_keep, col_keep = gather(front, delayed, dest[None, :], ids, dinv, linv)
+    columns, side_hi, side_lo, row_keep, col_keep = gather(
+        front, delayed, dest[None, :], pivots[None, :], pair_flags[None, :], dinv_diag[None, :], dinv_off[None, :], linv)
     trailing, factor = update(columns, side_hi, side_lo, front, row_keep, col_keep)
     return (trailing, factor)
 

time: 222 us -> 215 us (0.968)
  Pallas kernels: 218 us -> 214 us
  other arithmetic: 2.62 us -> 0 us
    pallas_call x1, Pallas kernels: 181 us -> 177 us  [gather(): pl.pallas_call(functools.partial(gather_kernel, (zs, xs, ys, halves, per_...]
    another operation x2 -> x0, other arithmetic: 2.62 us -> none  [the longest x1 1.31 us: body(): ids = jnp.stack([pivots, pair_flags])]
where the time goes in v4:
time: 215 us
  Pallas kernels  214 us (100%)
    pallas_call x1, Pallas kernels, gather(): pl.pallas_call(functools.partial(gather_kernel, (zs, xs, ys, halves, per_...  177 us
    pallas_call x1, Pallas kernels, update(): pl.pallas_call(trailing_kernel, grid=(rows // tile,), in_specs=[pl.BlockS...  37 us

profile of v4, /device:TPU:7, one launch (start us, length us, event | category | flops | bytes accessed | tf_op | source)
XLA Modules:
  0.0 214.9 jit_solution(5693710704858090656)
XLA Ops:
  0.6 177.2 %shard_map.95 = (f32[3072,1024]{1,0:T(8,128)}, bf16[1024,1536]{1,0:T(8,128)(2,1)}, bf16[1024,1536]{1,0:T(8,128)(2,1)}, f32[3072,1]{1,0:T(8,128)}, f32[1,1536]{1,0:T(1,128)}) custom-call(f32[3072,1536]{1,0:T(8,128)} %front_ref.3, f32[8,3072]{1,0:T(8,128)} %delayed_ref.1, s32[1,8]{1,0:T(1,128)} %bitcast.9, s32[1,1024]{1,0:T(1,128)} %bitcast.5, ...), custom_call_target="tpu_custom_call" | custom-call | tf_op jit(solution)/shard_map/pallas_call | solution.py:663
  177.9 37.0 %shard_map.96 = (f32[3072,1536]{1,0:T(8,128)}, f32[3072,1024]{1,0:T(8,128)}) custom-call(f32[3072,1024]{1,0:T(8,128)} %get-tuple-element.7.c_ref, bf16[1024,1536]{1,0:T(8,128)(2,1)} %get-tuple-element.8.hi_ref, bf16[1024,1536]{1,0:T(8,128)(2,1)} %get-tuple-element.9.lo_ref, f32[3072,1536]{1,0:T(8,128)} %front_ref.3, f32[3072,1]{1,0:T(8,128)} %get-tuple-element.10.rkeep_ref, ...), custom_call_target="tpu_custom_call" | custom-call | tf_op jit(solution)/shard_map/pallas_call | solution.py:730
